TPU v7x, 128 devices: a whole 4x4x4 slice. The times are simulated.
128 devices in a mesh: gx: 8 (over x, core), gy: 16 (over z, y).
Axes of the slice: x: 4, y: 4, z: 4, core: 2. Of those that a mesh axis runs over, the one named last changes fastest.
Arguments:
- phase: float32 [8, 32, 32, 32, 128], P('gx', 'gy'), may hold values from -1 to 1
- solute: float32 [8, 32, 32, 32, 128], P('gx', 'gy'), may hold values from -2.5 to 2.5
- undercool: float32 [8, 32], P('gx', 'gy'), may hold values from -0.5 to 0.5
- mobility: float32 [8, 32], P('gx', 'gy'), may hold values from 0.03 to 0.08
- diffusivity: float32 [8, 32], P('gx', 'gy'), may hold values from 0.04 to 0.14
- owner: int32 [8, 32], P('gx', 'gy'), may hold values from 0 to 127, as said below
Outputs:
- phase_out: float32 [128, 2, 32, 32, 128], P(('gx', 'gy'))
- solute_out: float32 [128, 2, 32, 32, 128], P(('gx', 'gy'))
Inputs may be any that keep to these rules, and one draw needn't show every extreme that they name: A tile (p, q) is owned by one of the owners i*16 to i*16+16-1 with i = p. Each owner receives exactly 2 tiles; no device's tiles include more than 1 tiles of one owner, and some device's include exactly 1.
All inputs are finite; a program needn't handle non-finite values.
Results may differ from a plain program's by a relative error of at most 0.0003.
Values sent between devices are 32-bit elements; how exact they have to be, the bound alone decides.
A program may use at most 192 MiB of HBM per device.

v0:
```python
import jax
import jax.numpy as jnp
from jax import lax
from jax.sharding import PartitionSpec as P

NSTEPS = 4


aniso_strength = 0.05
coupling = 2.0


def extended(block, sides, width):
    for axis, dim in sides:
        count = lax.axis_size(axis)
        forward = [(i, i + 1) for i in range(count - 1)]
        forward.append((count - 1, 0))
        backward = [(target, source) for source, target in forward]
        low = lax.ppermute(
            lax.slice_in_dim(block, block.shape[dim] - width, None, axis=dim), axis, forward
        )
        high = lax.ppermute(lax.slice_in_dim(block, 0, width, axis=dim), axis, backward)
        block = jnp.concatenate([low, block, high], axis=dim)
    return block


def step_cells(phase, solute, phase_near, solute_near, under, mobile, spread):
    lower_first, upper_first, lower_second, upper_second, lower_third, upper_third = phase_near
    slope_first = 0.5 * (upper_first - lower_first)
    slope_second = 0.5 * (upper_second - lower_second)
    slope_third = 0.5 * (upper_third - lower_third)
    lap_phase = (
        upper_first
        + lower_first
        + upper_second
        + lower_second
        + upper_third
        + lower_third
        - 6.0 * phase
    )
    sol_lf, sol_uf, sol_ls, sol_us, sol_lt, sol_ut = solute_near
    lap_solute = sol_uf + sol_lf + sol_us + sol_ls + sol_ut + sol_lt - 6.0 * solute
    square_first = slope_first * slope_first
    square_second = slope_second * slope_second
    square_third = slope_third * slope_third
    grad_two = square_first + square_second + square_third
    grad_four = (
        square_first * square_first + square_second * square_second + square_third * square_third
    )
    aniso = 1.0 + aniso_strength * (4.0 * grad_four - 3.0 * grad_two * grad_two) / (
        (1.0 + grad_two) * (1.0 + grad_two)
    )
    well = 1.0 - phase * phase
    new_phase = phase + mobile * (
        aniso * lap_phase
        + phase
        - phase * phase * phase
        - coupling * well * well * (under + solute)
    )
    new_solute = solute + spread * lap_solute + 0.5 * (new_phase - phase)
    return (new_phase, new_solute)


def neighbours(field, lower_x, upper_x, lower_y, upper_y):
    return (
        jnp.concatenate([lower_x[:, None], field[:, :-1]], 1),
        jnp.concatenate([field[:, 1:], upper_x[:, None]], 1),
        jnp.concatenate([lower_y[:, :, None], field[:, :, :-1]], 2),
        jnp.concatenate([field[:, :, 1:], upper_y[:, :, None]], 2),
        jnp.concatenate([field[..., :1], field[..., :-1]], 3),
        jnp.concatenate([field[..., 1:], field[..., -1:]], 3),
    )


def advance(phase, solute, halo_faces, coefficients):
    under = coefficients[:, 0][:, None, None, None]
    mobile = coefficients[:, 1][:, None, None, None]
    spread = coefficients[:, 2][:, None, None, None]
    phase_near = neighbours(
        phase, halo_faces[:, 0], halo_faces[:, 1], halo_faces[:, 2], halo_faces[:, 3]
    )
    solute_near = neighbours(
        solute, halo_faces[:, 4], halo_faces[:, 5], halo_faces[:, 6], halo_faces[:, 7]
    )
    return step_cells(phase, solute, phase_near, solute_near, under, mobile, spread)


def boundary_faces(phase, solute):
    return jnp.stack(
        [
            phase[:, 0],
            phase[:, -1],
            phase[:, :, 0],
            phase[:, :, -1],
            solute[:, 0],
            solute[:, -1],
            solute[:, :, 0],
            solute[:, :, -1],
        ],
        axis=1,
    )


def home_halos(grid_faces, block_x, block_y):
    padded = extended(grid_faces, (("gx", 0), ("gy", 1)), 1)
    before_x = padded[0:block_x, 1 : block_y + 1]
    after_x = padded[2 : block_x + 2, 1 : block_y + 1]
    before_y = padded[1 : block_x + 1, 0:block_y]
    after_y = padded[1 : block_x + 1, 2 : block_y + 2]
    gathered = jnp.stack(
        [
            before_x[:, :, 1],
            after_x[:, :, 0],
            before_y[:, :, 3],
            after_y[:, :, 2],
            before_x[:, :, 5],
            after_x[:, :, 4],
            before_y[:, :, 7],
            after_y[:, :, 6],
        ],
        axis=2,
    )
    return gathered.reshape((block_x * block_y,) + gathered.shape[2:])


def place(values, target, slots):
    return jnp.zeros((slots,) + values.shape[1:], values.dtype).at[target].set(values)


def pick_slots(present, tiles_here, slots):
    position = jnp.cumsum(present) - 1
    wanted = (position[None, :] == jnp.arange(tiles_here, dtype=jnp.int32)[:, None]) & (
        present[None, :] == 1
    )
    return jnp.sum(jnp.where(wanted, jnp.arange(slots, dtype=jnp.int32)[None, :], 0), axis=1)


def per_device(phase, solute, undercool, mobility, diffusivity, owner):
    block_x, block_y = owner.shape
    tiles_here = block_x * block_y
    edge = phase.shape[2]
    depth = phase.shape[4]
    mesh_y = lax.axis_size("gy")
    capacity = max(1, tiles_here // mesh_y)
    slots = mesh_y * capacity
    owner_flat = owner.reshape(tiles_here)
    peer = owner_flat % mesh_y
    matches = (peer[:, None] == jnp.arange(mesh_y, dtype=jnp.int32)[None, :]).astype(jnp.int32)
    earlier = jnp.cumsum(matches, axis=0) - matches
    sender_rank = jnp.sum(earlier * matches, axis=1)
    target = peer * capacity + sender_rank
    flag_send = jnp.zeros((slots,), jnp.int32).at[target].set(1)
    phase_tiles = phase.reshape(tiles_here, edge, edge, depth)
    solute_tiles = solute.reshape(tiles_here, edge, edge, depth)
    coefficients = jnp.stack(
        [
            undercool.reshape(tiles_here),
            mobility.reshape(tiles_here),
            diffusivity.reshape(tiles_here),
        ],
        axis=1,
    )
    grid_faces = boundary_faces(phase_tiles, solute_tiles).reshape(block_x, block_y, 8, edge, depth)
    first_halos = home_halos(grid_faces, block_x, block_y)
    arrived = (
        lax.all_to_all(
            place(phase_tiles, target, slots), "gy", split_axis=0, concat_axis=0, tiled=True
        ),
        lax.all_to_all(
            place(solute_tiles, target, slots), "gy", split_axis=0, concat_axis=0, tiled=True
        ),
        lax.all_to_all(
            place(coefficients, target, slots), "gy", split_axis=0, concat_axis=0, tiled=True
        ),
        lax.all_to_all(
            place(first_halos, target, slots), "gy", split_axis=0, concat_axis=0, tiled=True
        ),
        lax.all_to_all(flag_send, "gy", split_axis=0, concat_axis=0, tiled=True),
    )
    picked = pick_slots(arrived[4], tiles_here, slots)
    phase_owned = arrived[0][picked]
    solute_owned = arrived[1][picked]
    coeff_owned = arrived[2][picked]
    halo_owned = arrived[3][picked]
    for iteration in range(NSTEPS):
        if iteration > 0:
            returned = lax.all_to_all(
                place(boundary_faces(phase_owned, solute_owned), picked, slots),
                "gy",
                split_axis=0,
                concat_axis=0,
                tiled=True,
            )
            home_grid = returned[target].reshape(block_x, block_y, 8, edge, depth)
            outgoing = place(home_halos(home_grid, block_x, block_y), target, slots)
            halo_owned = lax.all_to_all(outgoing, "gy", split_axis=0, concat_axis=0, tiled=True)[
                picked
            ]
        phase_owned, solute_owned = advance(phase_owned, solute_owned, halo_owned, coeff_owned)
    return (
        phase_owned.reshape(1, tiles_here, edge, edge, depth),
        solute_owned.reshape(1, tiles_here, edge, edge, depth),
    )


def solution(mesh):
    in_specs = (
        P("gx", "gy", None, None, None),
        P("gx", "gy", None, None, None),
        P("gx", "gy"),
        P("gx", "gy"),
        P("gx", "gy"),
        P("gx", "gy"),
    )
    out_specs = (P(("gx", "gy"), None, None, None, None), P(("gx", "gy"), None, None, None, None))
    return jax.shard_map(
        per_device, mesh=mesh, in_specs=in_specs, out_specs=out_specs, check_vma=False
    )
```

profile of v0, /device:TPU:0, one launch (start us, length us, event | category | flops | bytes accessed | tf_op | source)
XLA Modules:
  0.0 680.9 jit_solution(18360599481350868769)
XLA Ops:
  2.9 2.9 collective-permute-start.1
  7.4 8.1 %all-to-all-start.1 = ((s32[16,1,1]{2,1,0:T(1,128)}), s32[16,1,1]{2,1,0:T(1,128)S(1)}, u32[]{:S(2)}, u32[]{:S(2)}) async-start(s32[16,1,1]{2,1,0:T(1,128)} %copy.623), calls=%async_computation.1 | async-start | bytes 16384 | tf_op jit(solution)/shard_map/all_to_all | solution.py:178
  19.0 3.4 collective-permute-start.3
  22.4 7.4 %collective-permute-done.2 = f32[3,1,8,32,128]{4,3,1,2,0:T(8,128)S(1)} collective-permute-done((f32[3,1,8,32,128]{4,3,1,2,0:T(8,128)S(1)}, f32[3,1,8,32,128]{4,3,1,2,0:T(8,128)S(1)}, u32[]{:S(2)}, u32[]{:S(2)}) %collective-permute-start.2) | collective-permute-done | bytes 393248 | tf_op jit(solution)/shard_map/ppermute | solution.py:19
  29.9 6.4 all-to-all-start.2
  40.1 3.6 all-to-all-done.2
  43.8 3.7 all-to-all-start.3
  47.5 4.4 broadcast.848.clone
  51.9 2.8 scatter_fusion.2
  54.7 20.2 %all-to-all-done.3 = f32[16,8,32,128]{3,2,1,0:T(8,128)S(1)} async-done(((f32[16,8,32,128]{3,2,1,0:T(8,128)}), f32[16,8,32,128]{3,2,1,0:T(8,128)S(1)}, u32[]{:S(2)}, u32[]{:S(2)}) %all-to-all-start.3) | async-done | bytes 2097184 | tf_op jit(solution)/shard_map/all_to_all | solution.py:175
  76.2 4.8 all-to-all-start.4
  81.0 4.4 broadcast.848.clone.1
  85.4 2.8 scatter_fusion
  88.2 108.0 %all-to-all-done.4 = f32[16,32,32,128]{3,2,1,0:T(8,128)} async-done(((f32[16,32,32,128]{3,2,1,0:T(8,128)}), f32[16,32,32,128]{3,2,1,0:T(8,128)}, u32[]{:S(2)}, u32[]{:S(2)}) %all-to-all-start.4) | async-done | bytes 8388640 | tf_op jit(solution)/shard_map/all_to_all | solution.py:169
  196.2 5.9 all-to-all-start
  206.9 4.0 gather_fusion.3
  213.2 2.4 fusion.181
  215.5 2.7 fusion.179
  218.2 2.6 fusion.180
  220.8 92.6 %all-to-all-done = f32[16,32,32,128]{3,2,1,0:T(8,128)} async-done(((f32[16,32,32,128]{3,2,1,0:T(8,128)}), f32[16,32,32,128]{3,2,1,0:T(8,128)}, u32[]{:S(2)}, u32[]{:S(2)}) %all-to-all-start) | async-done | bytes 8388640 | tf_op jit(solution)/shard_map/all_to_all | solution.py:166
  313.4 4.0 gather_fusion
  325.9 3.3 fusion.84
  332.0 2.4 scatter_fusion.3
  334.4 5.3 all-to-all-start.5
  340.3 25.0 %all-to-all-done.5 = f32[16,8,32,128]{3,2,1,0:T(8,128)} async-done(((f32[16,8,32,128]{3,2,1,0:T(8,128)}), f32[16,8,32,128]{3,2,1,0:T(8,128)}, u32[]{:S(2)}, u32[]{:S(2)}) %all-to-all-start.5) | async-done | bytes 2097184 | tf_op jit(solution)/shard_map/all_to_all | solution.py:187
  365.3 2.3 gather_fusion.4
  367.6 2.9 collective-permute-start.5
  370.5 4.1 collective-permute-done.4
  374.6 7.4 %collective-permute-done.5 = f32[1,2,8,32,128]{4,3,2,1,0:T(8,128)S(1)} collective-permute-done((f32[1,2,8,32,128]{4,3,2,1,0:T(8,128)S(1)}, f32[1,2,8,32,128]{4,3,2,1,0:T(8,128)S(1)}, u32[]{:S(2)}, u32[]{:S(2)}) %collective-permute-start.5) | collective-permute-done | bytes 262176 | tf_op jit(solution)/shard_map/ppermute | solution.py:22
  382.4 5.1 collective-permute-start.7
  387.6 5.8 collective-permute-done.6
  397.9 7.1 %all-to-all-start.6 = ((f32[16,8,32,128]{3,2,1,0:T(8,128)}), f32[16,8,32,128]{3,2,1,0:T(8,128)}, u32[]{:S(2)}, u32[]{:S(2)}) async-start(f32[16,8,32,128]{3,2,1,0:T(8,128)} %scatter_fusion.4), calls=%async_computation.6 | async-start | bytes 4194304 | tf_op jit(solution)/shard_map/all_to_all | solution.py:196
  405.0 5.3 fusion.165
  410.3 3.6 fusion.166
  413.9 4.2 fusion.168
  418.1 4.1 fusion.167
  422.2 11.2 %all-to-all-done.6 = f32[16,8,32,128]{3,2,1,0:T(8,128)} async-done(((f32[16,8,32,128]{3,2,1,0:T(8,128)}), f32[16,8,32,128]{3,2,1,0:T(8,128)}, u32[]{:S(2)}, u32[]{:S(2)}) %all-to-all-start.6) | async-done | bytes 2097184 | tf_op jit(solution)/shard_map/all_to_all | solution.py:196
  436.4 8.0 %fusion.100 = (f32[2,32,32,128]{3,2,1,0:T(8,128)S(1)}, f32[2,32,32,128]{3,2,1,0:T(8,128)S(1)}) fusion(f32[2,32,32,128]{3,2,1,0:T(8,128)} %copy-done.2, f32[2,1,32,128]{3,2,1,0:T(8,128)S(1)} %get-tuple-element.184, f32[2,31,32,128]{3,2,1,0:T(8,128)} %get-tuple-element.199, f32[2,31,32,128]{3,2,1,0:T(8,128)} %get-tuple-element.202, ...), kind=kLoop, calls=%fused_computation.188 | loop fusion | flops 18087936 | bytes 16777240 | tf_op jit(solution)/shard_map/add | solution.py:60
  447.1 2.4 scatter_fusion.5
  449.4 36.6 %all_to_all.66 = f32[16,8,32,128]{3,2,1,0:T(8,128)} all-to-all(f32[16,8,32,128]{3,2,1,0:T(8,128)} %scatter_fusion.5), channel_id=1, replica_groups=mesh['gx'=8,'gy'=16] {'gy'}, dimensions={0} | all-to-all | bytes 4194304 | tf_op jit(solution)/shard_map/all_to_all | solution.py:187
  488.4 2.8 collective-permute-start.9
  491.2 3.7 fusion.162
  496.1 4.8 collective-permute-start.11
  500.9 7.0 %collective-permute-done.10 = f32[3,1,8,32,128]{4,3,2,1,0:T(8,128)S(1)} collective-permute-done((f32[3,1,8,32,128]{4,3,2,1,0:T(8,128)S(1)}, f32[3,1,8,32,128]{4,3,2,1,0:T(8,128)S(1)}, u32[]{:S(2)}, u32[]{:S(2)}) %collective-permute-start.10) | collective-permute-done | bytes 393248 | tf_op jit(solution)/shard_map/ppermute | solution.py:19
  512.4 7.1 %all-to-all-start.8 = ((f32[16,8,32,128]{3,2,1,0:T(8,128)}), f32[16,8,32,128]{3,2,1,0:T(8,128)}, u32[]{:S(2)}, u32[]{:S(2)}) async-start(f32[16,8,32,128]{3,2,1,0:T(8,128)} %scatter_fusion.6), calls=%async_computation.8 | async-start | bytes 4194304 | tf_op jit(solution)/shard_map/all_to_all | solution.py:196
  524.0 2.6 fusion.159
  526.6 2.6 fusion.160
  529.2 2.5 fusion.157
  531.7 2.5 fusion.158
  534.2 2.5 fusion.156
  536.7 15.0 %all-to-all-done.8 = f32[16,8,32,128]{3,2,1,0:T(8,128)} async-done(((f32[16,8,32,128]{3,2,1,0:T(8,128)}), f32[16,8,32,128]{3,2,1,0:T(8,128)}, u32[]{:S(2)}, u32[]{:S(2)}) %all-to-all-start.8) | async-done | bytes 2097184 | tf_op jit(solution)/shard_map/all_to_all | solution.py:196
  554.7 7.7 %fusion.116 = (f32[2,32,32,128]{3,2,1,0:T(8,128)S(1)}, f32[2,32,32,128]{3,2,1,0:T(8,128)S(1)}) fusion(f32[2,32,32,128]{3,2,1,0:T(8,128)} %copy-done, f32[2,1,32,128]{3,2,1,0:T(8,128)S(1)} %get-tuple-element.170, f32[2,31,32,128]{3,2,1,0:T(8,128)} %get-tuple-element.70, f32[2,31,32,128]{3,2,1,0:T(8,128)} %get-tuple-element.67, ...), kind=kLoop, calls=%fused_computation.218 | loop fusion | flops 18087936 | bytes 16777240 | tf_op jit(solution)/shard_map/add | solution.py:60
  567.7 4.6 all-to-all-start.9
  572.6 7.2 %fusion.92 = (f32[1,2,32,32,128]{4,3,2,1,0:T(8,128)S(1)}, f32[1,2,32,32,128]{4,3,2,1,0:T(8,128)S(1)}) fusion(f32[1,2,1,32,128]{4,3,2,1,0:T(8,128)S(1)} %copy-done.75, f32[1,2,31,32,128]{4,3,2,1,0:T(8,128)} %get-tuple-element.140, f32[1,2,31,32,128]{4,3,2,1,0:T(8,128)} %get-tuple-element.141, f32[1,2,1,32,128]{4,3,2,1,0:T(8,128)S(1)} %copy-done.76, ...), kind=kLoop, calls=%fused_computation.173 | loop fusion | flops 18087936 | bytes 16777240 | tf_op jit(solution)/shard_map/add | solution.py:60
  582.7 4.7 fusion.108
  592.2 15.4 %all-to-all-done.9 = f32[16,8,32,128]{3,2,1,0:T(8,128)} async-done(((f32[16,8,32,128]{3,2,1,0:T(8,128)}), f32[16,8,32,128]{3,2,1,0:T(8,128)}, u32[]{:S(2)}, u32[]{:S(2)}) %all-to-all-start.9) | async-done | bytes 2097184 | tf_op jit(solution)/shard_map/all_to_all | solution.py:187
  610.0 2.8 collective-permute-start.13
  614.4 2.5 collective-permute-done.12
  617.1 5.3 collective-permute-start.15
  622.5 8.2 %collective-permute-done.14 = f32[3,1,8,32,128]{4,3,2,1,0:T(8,128)S(1)} collective-permute-done((f32[3,1,8,32,128]{4,3,2,1,0:T(8,128)S(1)}, f32[3,1,8,32,128]{4,3,2,1,0:T(8,128)S(1)}, u32[]{:S(2)}, u32[]{:S(2)}) %collective-permute-start.14) | collective-permute-done | bytes 393248 | tf_op jit(solution)/shard_map/ppermute | solution.py:19
  634.6 6.7 all-to-all-start.10
  650.2 5.2 fusion.124
  655.3 14.3 %all-to-all-done.10 = f32[16,8,32,128]{3,2,1,0:T(8,128)} async-done(((f32[16,8,32,128]{3,2,1,0:T(8,128)}), f32[16,8,32,128]{3,2,1,0:T(8,128)}, u32[]{:S(2)}, u32[]{:S(2)}) %all-to-all-start.10) | async-done | bytes 2097184 | tf_op jit(solution)/shard_map/all_to_all | solution.py:196
  672.0 8.7 %fusion.132 = (f32[1,2,32,32,128]{4,3,2,1,0:T(8,128)}, f32[1,2,32,32,128]{4,3,2,1,0:T(8,128)}) fusion(f32[1,2,32,32,128]{4,3,2,1,0:T(8,128)S(1)} %get-tuple-element.9, f32[1,2,1,32,128]{4,3,2,1,0:T(8,128)S(1)} %get-tuple-element.158, f32[1,2,31,32,128]{4,3,2,1,0:T(8,128)} %get-tuple-element.34, f32[1,2,31,32,128]{4,3,2,1,0:T(8,128)} %get-tuple-element.33, ...), kind=kLoop, calls=%fused_computation.242 | loop fusion | flops 18087936 | bytes 16777240 | tf_op jit(solution)/shard_map/add | solution.py:60
  (343 shorter events, 89.1 us)
Async XLA Ops:
  0.7 14.9 %copy-start.88 = (f32[1,2]{1,0:T(1,128)S(1)}, f32[1,2]{1,0:T(1,128)}, u32[]{:S(2)}) copy-start(f32[1,2]{1,0:T(1,128)} %param.10) | copy-start | bytes 28
  0.7 14.9 %copy-start.89 = (f32[1,2]{1,0:T(1,128)S(1)}, f32[1,2]{1,0:T(1,128)}, u32[]{:S(2)}) copy-start(f32[1,2]{1,0:T(1,128)} %param.9) | copy-start | bytes 28
  0.7 14.9 %copy-start.90 = (f32[1,2]{1,0:T(1,128)S(1)}, f32[1,2]{1,0:T(1,128)}, u32[]{:S(2)}) copy-start(f32[1,2]{1,0:T(1,128)} %param.8) | copy-start | bytes 28
  2.8 14.0 %collective-permute-start = (f32[1,2,8,32,128]{4,3,1,2,0:T(8,128)S(1)}, f32[1,2,8,32,128]{4,3,1,2,0:T(8,128)S(1)}, u32[]{:S(2)}, u32[]{:S(2)}) collective-permute-start(f32[1,2,8,32,128]{4,3,1,2,0:T(8,128)S(1)} %bitcast.485), channel_id=1, source_target_pairs={{0,16},{16,32},{32,48},{48,64},{64,80},{80,96},{96,112},{112,0},{1... | collective-permute-start | bytes 786440 | tf_op jit(solution)/shard_map/ppermute | solution.py:19
  2.9 14.0 %collective-permute-start.1 = (f32[1,2,8,32,128]{4,3,1,2,0:T(8,128)S(1)}, f32[1,2,8,32,128]{4,3,1,2,0:T(8,128)S(1)}, u32[]{:S(2)}, u32[]{:S(2)}) collective-permute-start(f32[1,2,8,32,128]{4,3,1,2,0:T(8,128)S(1)} %bitcast.486), channel_id=1, source_target_pairs={{16,0},{32,16},{48,32},{64,48},{80,64},{96,80},{112,96},{0,112},{1... | collective-permute-start | bytes 786440 | tf_op jit(solution)/shard_map/ppermute | solution.py:22
  7.4 22.5 %all-to-all-start.1 = ((s32[16,1,1]{2,1,0:T(1,128)}), s32[16,1,1]{2,1,0:T(1,128)S(1)}, u32[]{:S(2)}, u32[]{:S(2)}) async-start(s32[16,1,1]{2,1,0:T(1,128)} %copy.623), calls=%async_computation.1 | async-start | bytes 16384 | tf_op jit(solution)/shard_map/all_to_all | solution.py:178
  17.0 12.8 %collective-permute-start.2 = (f32[3,1,8,32,128]{4,3,1,2,0:T(8,128)S(1)}, f32[3,1,8,32,128]{4,3,1,2,0:T(8,128)S(1)}, u32[]{:S(2)}, u32[]{:S(2)}) collective-permute-start(f32[3,1,8,32,128]{4,3,1,2,0:T(8,128)S(1)} %get-tuple-element.154), channel_id=1, source_target_pairs={{0,1},{1,2},{2,3},{3,4},{4,5},{5,6},{6,7},{7,8},{8,9},{9,10},{10,1... | collective-permute-start | bytes 1179656 | tf_op jit(solution)/shard_map/ppermute | solution.py:19
  19.0 10.8 %collective-permute-start.3 = (f32[3,1,8,32,128]{4,3,1,2,0:T(8,128)S(1)}, f32[3,1,8,32,128]{4,3,1,2,0:T(8,128)S(1)}, u32[]{:S(2)}, u32[]{:S(2)}) collective-permute-start(f32[3,1,8,32,128]{4,3,1,2,0:T(8,128)S(1)} %get-tuple-element.153), channel_id=1, source_target_pairs={{1,0},{2,1},{3,2},{4,3},{5,4},{6,5},{7,6},{8,7},{9,8},{10,9},{11,1... | collective-permute-start | bytes 1179656 | tf_op jit(solution)/shard_map/ppermute | solution.py:22
  29.9 13.9 %all-to-all-start.2 = ((f32[16,1,3]{2,1,0:T(1,128)}), f32[16,1,3]{2,1,0:T(1,128)S(1)}, u32[]{:S(2)}, u32[]{:S(2)}) async-start(f32[16,1,3]{2,1,0:T(1,128)} %bitcast.174), calls=%async_computation.2 | async-start | bytes 16384 | tf_op jit(solution)/shard_map/all_to_all | solution.py:172
  43.8 31.1 %all-to-all-start.3 = ((f32[16,8,32,128]{3,2,1,0:T(8,128)}), f32[16,8,32,128]{3,2,1,0:T(8,128)S(1)}, u32[]{:S(2)}, u32[]{:S(2)}) async-start(f32[16,8,32,128]{3,2,1,0:T(8,128)} %scatter_fusion.1), calls=%async_computation.3 | async-start | bytes 4194304 | tf_op jit(solution)/shard_map/all_to_all | solution.py:175
  76.2 120.0 %all-to-all-start.4 = ((f32[16,32,32,128]{3,2,1,0:T(8,128)}), f32[16,32,32,128]{3,2,1,0:T(8,128)}, u32[]{:S(2)}, u32[]{:S(2)}) async-start(f32[16,32,32,128]{3,2,1,0:T(8,128)} %scatter_fusion.2), calls=%async_computation.4 | async-start | bytes 16777216 | tf_op jit(solution)/shard_map/all_to_all | solution.py:169
  196.2 117.2 %all-to-all-start = ((f32[16,32,32,128]{3,2,1,0:T(8,128)}), f32[16,32,32,128]{3,2,1,0:T(8,128)}, u32[]{:S(2)}, u32[]{:S(2)}) async-start(f32[16,32,32,128]{3,2,1,0:T(8,128)} %scatter_fusion), calls=%async_computation | async-start | bytes 16777216 | tf_op jit(solution)/shard_map/all_to_all | solution.py:166
  203.3 110.1 %copy-start.85 = (s32[1024]{0:T(1024)}, s32[1024]{0:T(1024)S(1)}, u32[]{:S(2)}) copy-start(s32[1024]{0:T(1024)S(1)} %pad_clamp_fusion.1) | copy-start | bytes 12292
  329.2 88.9 %copy-start.2 = (f32[2,32,32,128]{3,2,1,0:T(8,128)}, f32[2,32,32,128]{3,2,1,0:T(8,128)S(1)}, u32[]{:S(2)}) copy-start(f32[2,32,32,128]{3,2,1,0:T(8,128)S(1)} %get-tuple-element.15) | copy-start | bytes 3145732
  334.4 30.9 %all-to-all-start.5 = ((f32[16,8,32,128]{3,2,1,0:T(8,128)}), f32[16,8,32,128]{3,2,1,0:T(8,128)}, u32[]{:S(2)}, u32[]{:S(2)}) async-start(f32[16,8,32,128]{3,2,1,0:T(8,128)} %scatter_fusion.3), calls=%async_computation.5 | async-start | bytes 4194304 | tf_op jit(solution)/shard_map/all_to_all | solution.py:187
  367.6 7.0 %collective-permute-start.4 = (f32[1,2,8,32,128]{4,3,2,1,0:T(8,128)S(1)}, f32[1,2,8,32,128]{4,3,2,1,0:T(8,128)S(1)}, u32[]{:S(2)}, u32[]{:S(2)}) collective-permute-start(f32[1,2,8,32,128]{4,3,2,1,0:T(8,128)S(1)} %bitcast.478), channel_id=1, source_target_pairs={{0,16},{16,32},{32,48},{48,64},{64,80},{80,96},{96,112},{112,0},{1... | collective-permute-start | bytes 786440 | tf_op jit(solution)/shard_map/ppermute | solution.py:19
  367.6 14.4 %collective-permute-start.5 = (f32[1,2,8,32,128]{4,3,2,1,0:T(8,128)S(1)}, f32[1,2,8,32,128]{4,3,2,1,0:T(8,128)S(1)}, u32[]{:S(2)}, u32[]{:S(2)}) collective-permute-start(f32[1,2,8,32,128]{4,3,2,1,0:T(8,128)S(1)} %bitcast.479), channel_id=1, source_target_pairs={{16,0},{32,16},{48,32},{64,48},{80,64},{96,80},{112,96},{0,112},{1... | collective-permute-start | bytes 786440 | tf_op jit(solution)/shard_map/ppermute | solution.py:22
  382.1 11.2 %collective-permute-start.6 = (f32[3,1,8,32,128]{4,3,2,1,0:T(8,128)S(1)}, f32[3,1,8,32,128]{4,3,2,1,0:T(8,128)S(1)}, u32[]{:S(2)}, u32[]{:S(2)}) collective-permute-start(f32[3,1,8,32,128]{4,3,2,1,0:T(8,128)S(1)} %get-tuple-element.152), channel_id=1, source_target_pairs={{0,1},{1,2},{2,3},{3,4},{4,5},{5,6},{6,7},{7,8},{8,9},{9,10},{10,1... | collective-permute-start | bytes 1179656 | tf_op jit(solution)/shard_map/ppermute | solution.py:19
  382.4 10.9 %collective-permute-start.7 = (f32[3,1,8,32,128]{4,3,2,1,0:T(8,128)S(1)}, f32[3,1,8,32,128]{4,3,2,1,0:T(8,128)S(1)}, u32[]{:S(2)}, u32[]{:S(2)}) collective-permute-start(f32[3,1,8,32,128]{4,3,2,1,0:T(8,128)S(1)} %get-tuple-element.151), channel_id=1, source_target_pairs={{1,0},{2,1},{3,2},{4,3},{5,4},{6,5},{7,6},{8,7},{9,8},{10,9},{11,1... | collective-permute-start | bytes 1179656 | tf_op jit(solution)/shard_map/ppermute | solution.py:22
  397.9 35.5 %all-to-all-start.6 = ((f32[16,8,32,128]{3,2,1,0:T(8,128)}), f32[16,8,32,128]{3,2,1,0:T(8,128)}, u32[]{:S(2)}, u32[]{:S(2)}) async-start(f32[16,8,32,128]{3,2,1,0:T(8,128)} %scatter_fusion.4), calls=%async_computation.6 | async-start | bytes 4194304 | tf_op jit(solution)/shard_map/all_to_all | solution.py:196
  436.4 8.0 %copy-start.57 = (f32[2,1,32,128]{3,2,1,0:T(8,128)}, f32[2,1,32,128]{3,2,1,0:T(8,128)S(1)}, u32[]{:S(2)}) copy-start(f32[2,1,32,128]{3,2,1,0:T(8,128)S(1)} %get-tuple-element.180) | copy-start | bytes 98308
  436.4 8.0 %copy-start.59 = (f32[2,1,32,128]{3,2,1,0:T(8,128)}, f32[2,1,32,128]{3,2,1,0:T(8,128)S(1)}, u32[]{:S(2)}) copy-start(f32[2,1,32,128]{3,2,1,0:T(8,128)S(1)} %get-tuple-element.181) | copy-start | bytes 98308
  436.4 8.0 %copy-start.61 = (f32[2,1,32,128]{3,2,1,0:T(8,128)}, f32[2,1,32,128]{3,2,1,0:T(8,128)S(1)}, u32[]{:S(2)}) copy-start(f32[2,1,32,128]{3,2,1,0:T(8,128)S(1)} %get-tuple-element.182) | copy-start | bytes 98308
  436.4 8.0 %copy-start.63 = (f32[2,1,32,128]{3,2,1,0:T(8,128)}, f32[2,1,32,128]{3,2,1,0:T(8,128)S(1)}, u32[]{:S(2)}) copy-start(f32[2,1,32,128]{3,2,1,0:T(8,128)S(1)} %get-tuple-element.185) | copy-start | bytes 98308
  488.3 7.0 %collective-permute-start.8 = (f32[1,2,8,32,128]{4,3,2,1,0:T(8,128)S(1)}, f32[1,2,8,32,128]{4,3,2,1,0:T(8,128)S(1)}, u32[]{:S(2)}, u32[]{:S(2)}) collective-permute-start(f32[1,2,8,32,128]{4,3,2,1,0:T(8,128)S(1)} %bitcast.464), channel_id=1, source_target_pairs={{0,16},{16,32},{32,48},{48,64},{64,80},{80,96},{96,112},{112,0},{1... | collective-permute-start | bytes 786440 | tf_op jit(solution)/shard_map/ppermute | solution.py:19
  488.4 6.9 %collective-permute-start.9 = (f32[1,2,8,32,128]{4,3,2,1,0:T(8,128)S(1)}, f32[1,2,8,32,128]{4,3,2,1,0:T(8,128)S(1)}, u32[]{:S(2)}, u32[]{:S(2)}) collective-permute-start(f32[1,2,8,32,128]{4,3,2,1,0:T(8,128)S(1)} %bitcast.465), channel_id=1, source_target_pairs={{16,0},{32,16},{48,32},{64,48},{80,64},{96,80},{112,96},{0,112},{1... | collective-permute-start | bytes 786440 | tf_op jit(solution)/shard_map/ppermute | solution.py:22
  495.4 12.4 %collective-permute-start.10 = (f32[3,1,8,32,128]{4,3,2,1,0:T(8,128)S(1)}, f32[3,1,8,32,128]{4,3,2,1,0:T(8,128)S(1)}, u32[]{:S(2)}, u32[]{:S(2)}) collective-permute-start(f32[3,1,8,32,128]{4,3,2,1,0:T(8,128)S(1)} %get-tuple-element.150), channel_id=1, source_target_pairs={{0,1},{1,2},{2,3},{3,4},{4,5},{5,6},{6,7},{7,8},{8,9},{9,10},{10,1... | collective-permute-start | bytes 1179656 | tf_op jit(solution)/shard_map/ppermute | solution.py:19
  496.1 11.8 %collective-permute-start.11 = (f32[3,1,8,32,128]{4,3,2,1,0:T(8,128)S(1)}, f32[3,1,8,32,128]{4,3,2,1,0:T(8,128)S(1)}, u32[]{:S(2)}, u32[]{:S(2)}) collective-permute-start(f32[3,1,8,32,128]{4,3,2,1,0:T(8,128)S(1)} %get-tuple-element.149), channel_id=1, source_target_pairs={{1,0},{2,1},{3,2},{4,3},{5,4},{6,5},{7,6},{8,7},{9,8},{10,9},{11,1... | collective-permute-start | bytes 1179656 | tf_op jit(solution)/shard_map/ppermute | solution.py:22
  512.4 39.3 %all-to-all-start.8 = ((f32[16,8,32,128]{3,2,1,0:T(8,128)}), f32[16,8,32,128]{3,2,1,0:T(8,128)}, u32[]{:S(2)}, u32[]{:S(2)}) async-start(f32[16,8,32,128]{3,2,1,0:T(8,128)} %scatter_fusion.6), calls=%async_computation.8 | async-start | bytes 4194304 | tf_op jit(solution)/shard_map/all_to_all | solution.py:196
  554.7 7.7 %copy-start.65 = (f32[2,1,32,128]{3,2,1,0:T(8,128)}, f32[2,1,32,128]{3,2,1,0:T(8,128)S(1)}, u32[]{:S(2)}) copy-start(f32[2,1,32,128]{3,2,1,0:T(8,128)S(1)} %get-tuple-element.168) | copy-start | bytes 98308
  554.7 7.7 %copy-start.67 = (f32[2,1,32,128]{3,2,1,0:T(8,128)}, f32[2,1,32,128]{3,2,1,0:T(8,128)S(1)}, u32[]{:S(2)}) copy-start(f32[2,1,32,128]{3,2,1,0:T(8,128)S(1)} %get-tuple-element.171) | copy-start | bytes 98308
  554.7 7.7 %copy-start.69 = (f32[2,1,32,128]{3,2,1,0:T(8,128)}, f32[2,1,32,128]{3,2,1,0:T(8,128)S(1)}, u32[]{:S(2)}) copy-start(f32[2,1,32,128]{3,2,1,0:T(8,128)S(1)} %get-tuple-element.172) | copy-start | bytes 98308
  554.7 7.7 %copy-start.71 = (f32[2,1,32,128]{3,2,1,0:T(8,128)}, f32[2,1,32,128]{3,2,1,0:T(8,128)S(1)}, u32[]{:S(2)}) copy-start(f32[2,1,32,128]{3,2,1,0:T(8,128)S(1)} %get-tuple-element.174) | copy-start | bytes 98308
  567.7 39.9 %all-to-all-start.9 = ((f32[16,8,32,128]{3,2,1,0:T(8,128)}), f32[16,8,32,128]{3,2,1,0:T(8,128)}, u32[]{:S(2)}, u32[]{:S(2)}) async-start(f32[16,8,32,128]{3,2,1,0:T(8,128)} %scatter_fusion.7), calls=%async_computation.9 | async-start | bytes 4194304 | tf_op jit(solution)/shard_map/all_to_all | solution.py:187
  572.4 7.9 %copy-start.16 = (f32[1,2,32,32,1]{4,3,2,1,0:T(8,128)S(1)}, f32[1,2,32,32,1]{4,3,2,1,0:T(8,128)}, u32[]{:S(2)}) copy-start(f32[1,2,32,32,1]{4,3,2,1,0:T(8,128)} %get-tuple-element.213) | copy-start | bytes 24580
  572.4 8.2 %copy-start.17 = (f32[1,2,32,32,127]{4,3,2,1,0:T(8,128)S(1)}, f32[1,2,32,32,127]{4,3,2,1,0:T(8,128)}, u32[]{:S(2)}) copy-start(f32[1,2,32,32,127]{4,3,2,1,0:T(8,128)} %get-tuple-element.84) | copy-start | bytes 3121156
  572.4 8.4 %copy-start.18 = (f32[1,2,32,32,127]{4,3,2,1,0:T(8,128)S(1)}, f32[1,2,32,32,127]{4,3,2,1,0:T(8,128)}, u32[]{:S(2)}) copy-start(f32[1,2,32,32,127]{4,3,2,1,0:T(8,128)} %get-tuple-element.85) | copy-start | bytes 3121156
  572.4 8.7 %copy-start.19 = (f32[1,2,32,32,127]{4,3,2,1,0:T(8,128)S(1)}, f32[1,2,32,32,127]{4,3,2,1,0:T(8,128)}, u32[]{:S(2)}) copy-start(f32[1,2,32,32,127]{4,3,2,1,0:T(8,128)} %get-tuple-element.208) | copy-start | bytes 3121156
  572.4 9.0 %copy-start.20 = (f32[1,2,32,32,127]{4,3,2,1,0:T(8,128)S(1)}, f32[1,2,32,32,127]{4,3,2,1,0:T(8,128)}, u32[]{:S(2)}) copy-start(f32[1,2,32,32,127]{4,3,2,1,0:T(8,128)} %get-tuple-element.209) | copy-start | bytes 3121156
  572.4 9.3 %copy-start.44 = (f32[1,2,31,32,128]{4,3,2,1,0:T(8,128)S(1)}, f32[1,2,31,32,128]{4,3,2,1,0:T(8,128)}, u32[]{:S(2)}) copy-start(f32[1,2,31,32,128]{4,3,2,1,0:T(8,128)} %get-tuple-element.76) | copy-start | bytes 3047428
  572.5 9.6 %copy-start.45 = (f32[1,2,31,32,128]{4,3,2,1,0:T(8,128)S(1)}, f32[1,2,31,32,128]{4,3,2,1,0:T(8,128)}, u32[]{:S(2)}) copy-start(f32[1,2,31,32,128]{4,3,2,1,0:T(8,128)} %get-tuple-element.77) | copy-start | bytes 3047428
  572.5 9.9 %copy-start.46 = (f32[1,2,31,32,128]{4,3,2,1,0:T(8,128)S(1)}, f32[1,2,31,32,128]{4,3,2,1,0:T(8,128)}, u32[]{:S(2)}) copy-start(f32[1,2,31,32,128]{4,3,2,1,0:T(8,128)} %get-tuple-element.200) | copy-start | bytes 3047428
  572.5 10.2 %copy-start.47 = (f32[1,2,31,32,128]{4,3,2,1,0:T(8,128)S(1)}, f32[1,2,31,32,128]{4,3,2,1,0:T(8,128)}, u32[]{:S(2)}) copy-start(f32[1,2,31,32,128]{4,3,2,1,0:T(8,128)} %get-tuple-element.201) | copy-start | bytes 3047428
  572.5 10.1 %copy-start.58 = (f32[2,1,32,128]{3,2,1,0:T(8,128)S(1)}, f32[2,1,32,128]{3,2,1,0:T(8,128)}, u32[]{:S(2)}) copy-start(f32[2,1,32,128]{3,2,1,0:T(8,128)} %copy-done.57) | copy-start | bytes 98308
  572.5 10.1 %copy-start.60 = (f32[2,1,32,128]{3,2,1,0:T(8,128)S(1)}, f32[2,1,32,128]{3,2,1,0:T(8,128)}, u32[]{:S(2)}) copy-start(f32[2,1,32,128]{3,2,1,0:T(8,128)} %copy-done.59) | copy-start | bytes 98308
  572.5 10.1 %copy-start.62 = (f32[2,1,32,128]{3,2,1,0:T(8,128)S(1)}, f32[2,1,32,128]{3,2,1,0:T(8,128)}, u32[]{:S(2)}) copy-start(f32[2,1,32,128]{3,2,1,0:T(8,128)} %copy-done.61) | copy-start | bytes 98308
  572.5 10.1 %copy-start.64 = (f32[2,1,32,128]{3,2,1,0:T(8,128)S(1)}, f32[2,1,32,128]{3,2,1,0:T(8,128)}, u32[]{:S(2)}) copy-start(f32[2,1,32,128]{3,2,1,0:T(8,128)} %copy-done.63) | copy-start | bytes 98308
  572.5 10.1 %copy-start.77 = (f32[1,2,1,32,128]{4,3,2,1,0:T(8,128)S(1)}, f32[1,2,1,32,128]{4,3,2,1,0:T(8,128)}, u32[]{:S(2)}) copy-start(f32[1,2,1,32,128]{4,3,2,1,0:T(8,128)} %get-tuple-element.176) | copy-start | bytes 98308
  572.5 10.1 %copy-start.78 = (f32[1,2,1,32,128]{4,3,2,1,0:T(8,128)S(1)}, f32[1,2,1,32,128]{4,3,2,1,0:T(8,128)}, u32[]{:S(2)}) copy-start(f32[1,2,1,32,128]{4,3,2,1,0:T(8,128)} %get-tuple-element.177) | copy-start | bytes 98308
  572.5 10.1 %copy-start.79 = (f32[1,2,1,32,128]{4,3,2,1,0:T(8,128)S(1)}, f32[1,2,1,32,128]{4,3,2,1,0:T(8,128)}, u32[]{:S(2)}) copy-start(f32[1,2,1,32,128]{4,3,2,1,0:T(8,128)} %get-tuple-element.178) | copy-start | bytes 98308
  572.6 10.1 %copy-start.80 = (f32[1,2,1,32,128]{4,3,2,1,0:T(8,128)S(1)}, f32[1,2,1,32,128]{4,3,2,1,0:T(8,128)}, u32[]{:S(2)}) copy-start(f32[1,2,1,32,128]{4,3,2,1,0:T(8,128)} %get-tuple-element.179) | copy-start | bytes 98308
  609.9 7.0 %collective-permute-start.12 = (f32[1,2,8,32,128]{4,3,2,1,0:T(8,128)S(1)}, f32[1,2,8,32,128]{4,3,2,1,0:T(8,128)S(1)}, u32[]{:S(2)}, u32[]{:S(2)}) collective-permute-start(f32[1,2,8,32,128]{4,3,2,1,0:T(8,128)S(1)} %bitcast.471), channel_id=1, source_target_pairs={{0,16},{16,32},{32,48},{48,64},{64,80},{80,96},{96,112},{112,0},{1... | collective-permute-start | bytes 786440 | tf_op jit(solution)/shard_map/ppermute | solution.py:19
  610.0 6.9 %collective-permute-start.13 = (f32[1,2,8,32,128]{4,3,2,1,0:T(8,128)S(1)}, f32[1,2,8,32,128]{4,3,2,1,0:T(8,128)S(1)}, u32[]{:S(2)}, u32[]{:S(2)}) collective-permute-start(f32[1,2,8,32,128]{4,3,2,1,0:T(8,128)S(1)} %bitcast.472), channel_id=1, source_target_pairs={{16,0},{32,16},{48,32},{64,48},{80,64},{96,80},{112,96},{0,112},{1... | collective-permute-start | bytes 786440 | tf_op jit(solution)/shard_map/ppermute | solution.py:22
  617.0 13.6 %collective-permute-start.14 = (f32[3,1,8,32,128]{4,3,2,1,0:T(8,128)S(1)}, f32[3,1,8,32,128]{4,3,2,1,0:T(8,128)S(1)}, u32[]{:S(2)}, u32[]{:S(2)}) collective-permute-start(f32[3,1,8,32,128]{4,3,2,1,0:T(8,128)S(1)} %get-tuple-element.148), channel_id=1, source_target_pairs={{0,1},{1,2},{2,3},{3,4},{4,5},{5,6},{6,7},{7,8},{8,9},{9,10},{10,1... | collective-permute-start | bytes 1179656 | tf_op jit(solution)/shard_map/ppermute | solution.py:19
  617.1 13.6 %collective-permute-start.15 = (f32[3,1,8,32,128]{4,3,2,1,0:T(8,128)S(1)}, f32[3,1,8,32,128]{4,3,2,1,0:T(8,128)S(1)}, u32[]{:S(2)}, u32[]{:S(2)}) collective-permute-start(f32[3,1,8,32,128]{4,3,2,1,0:T(8,128)S(1)} %get-tuple-element.147), channel_id=1, source_target_pairs={{1,0},{2,1},{3,2},{4,3},{5,4},{6,5},{7,6},{8,7},{9,8},{10,9},{11,1... | collective-permute-start | bytes 1179656 | tf_op jit(solution)/shard_map/ppermute | solution.py:22
  634.6 13.4 %copy-start.66 = (f32[2,1,32,128]{3,2,1,0:T(8,128)S(1)}, f32[2,1,32,128]{3,2,1,0:T(8,128)}, u32[]{:S(2)}) copy-start(f32[2,1,32,128]{3,2,1,0:T(8,128)} %copy-done.65) | copy-start | bytes 98308
  634.6 13.4 %copy-start.68 = (f32[2,1,32,128]{3,2,1,0:T(8,128)S(1)}, f32[2,1,32,128]{3,2,1,0:T(8,128)}, u32[]{:S(2)}) copy-start(f32[2,1,32,128]{3,2,1,0:T(8,128)} %copy-done.67) | copy-start | bytes 98308
  634.6 13.4 %copy-start.70 = (f32[2,1,32,128]{3,2,1,0:T(8,128)S(1)}, f32[2,1,32,128]{3,2,1,0:T(8,128)}, u32[]{:S(2)}) copy-start(f32[2,1,32,128]{3,2,1,0:T(8,128)} %copy-done.69) | copy-start | bytes 98308
  634.6 13.4 %copy-start.72 = (f32[2,1,32,128]{3,2,1,0:T(8,128)S(1)}, f32[2,1,32,128]{3,2,1,0:T(8,128)}, u32[]{:S(2)}) copy-start(f32[2,1,32,128]{3,2,1,0:T(8,128)} %copy-done.71) | copy-start | bytes 98308
  634.6 13.4 %copy-start.81 = (f32[1,2,1,32,128]{4,3,2,1,0:T(8,128)S(1)}, f32[1,2,1,32,128]{4,3,2,1,0:T(8,128)}, u32[]{:S(2)}) copy-start(f32[1,2,1,32,128]{4,3,2,1,0:T(8,128)} %get-tuple-element.164) | copy-start | bytes 98308
  634.6 13.4 %copy-start.82 = (f32[1,2,1,32,128]{4,3,2,1,0:T(8,128)S(1)}, f32[1,2,1,32,128]{4,3,2,1,0:T(8,128)}, u32[]{:S(2)}) copy-start(f32[1,2,1,32,128]{4,3,2,1,0:T(8,128)} %get-tuple-element.165) | copy-start | bytes 98308
  634.6 13.4 %copy-start.83 = (f32[1,2,1,32,128]{4,3,2,1,0:T(8,128)S(1)}, f32[1,2,1,32,128]{4,3,2,1,0:T(8,128)}, u32[]{:S(2)}) copy-start(f32[1,2,1,32,128]{4,3,2,1,0:T(8,128)} %get-tuple-element.166) | copy-start | bytes 98308
  634.6 13.4 %copy-start.84 = (f32[1,2,1,32,128]{4,3,2,1,0:T(8,128)S(1)}, f32[1,2,1,32,128]{4,3,2,1,0:T(8,128)}, u32[]{:S(2)}) copy-start(f32[1,2,1,32,128]{4,3,2,1,0:T(8,128)} %get-tuple-element.167) | copy-start | bytes 98308
  634.6 35.1 %all-to-all-start.10 = ((f32[16,8,32,128]{3,2,1,0:T(8,128)}), f32[16,8,32,128]{3,2,1,0:T(8,128)}, u32[]{:S(2)}, u32[]{:S(2)}) async-start(f32[16,8,32,128]{3,2,1,0:T(8,128)} %scatter_fusion.8), calls=%async_computation.10 | async-start | bytes 4194304 | tf_op jit(solution)/shard_map/all_to_all | solution.py:196
  (54 other events, 218.2 us)
where the time goes:
time: 681 us
  waiting for transfers between devices  348 us (51%)
  local copies, waits for them, and re-layouts  154 us (23%)
  starting transfers between devices  93.2 us (14%)
  other arithmetic  46.6 us (7%)
  blocking collectives  36.6 us (5%)
    all_to_all x1, waiting for transfers between devices, per_device(): lax.all_to_all(place(solute_tiles, target, slots), 'gy', split_axis=0, co...  108 us
    all_to_all x1, waiting for transfers between devices, per_device(): lax.all_to_all(place(phase_tiles, target, slots), 'gy', split_axis=0, con...  92.6 us
    add x7, other arithmetic, step_cells(): new_solute = solute + spread * lap_solute + 0.5 * (new_phase - phase)  44.7 us
    all_to_all x3, waiting for transfers between devices, per_device(): lax.all_to_all(outgoing, 'gy', split_axis=0, concat_axis=0, tiled=True)  40.6 us
    all_to_all x2, waiting for transfers between devices, per_device(): lax.all_to_all(place(boundary_faces(phase_owned, solute_owned), picked, s...  40.4 us
    all_to_all x1, blocking collectives, per_device(): lax.all_to_all(place(boundary_faces(phase_owned, solute_owned), picked, s...  36.6 us
    ppermute x8, waiting for transfers between devices, extended(): lax.ppermute(lax.slice_in_dim(block, block.shape[dim] - width, None, axis...  35.2 us
    ppermute x8, starting transfers between devices, extended(): lax.ppermute(lax.slice_in_dim(block, 0, width, axis=dim), axis, backward)  30.2 us
  transfers between devices with their start and end apart: 26, of which 17 were waited for; matrix products, arithmetic and copies ran while one was open for 16% of the time, Pallas kernels for 0%

commit v1 on v0

v1 whole, which is shorter than its diff:
```python
import functools

import jax
import jax.numpy as jnp
from jax import lax
from jax.experimental import pallas as pl
from jax.experimental.pallas import tpu as pltpu
from jax.sharding import PartitionSpec as P

MESH = pl.DeviceIdType.MESH
NSTEPS = 4
RIM = 4
EDGE = 32
DEPTH = 128
GROUPS = 10
CHUNKS = 8
ORDER = (1, 2, 3, 4, 5, 6, 0, 7)

aniso_strength = 0.05
coupling = 2.0


def kernel(
    n_gx, n_gy,
    phase, solute, under_s, mobile_s, spread_s, owner_s,
    out,
    lev, fin, halo, coef, own, ownid, ids, table_v, table_s, stage,
    recv0, recv1, recv2, recv3, recv4, recv5, recv6, recv7,
    in_sem, y_sem, x_sem, c_sem, coef_sem, id_sem, tab_sem, hop1_sem, out_sem,
    halo_send, coef_send, id_send, hop1_send, hop2_send,
):
    recv = (recv0, recv1, recv2, recv3, recv4, recv5, recv6, recv7)
    fields = (phase, solute)
    gx = lax.axis_index("gx")
    gy = lax.axis_index("gy")
    gx_up = lax.rem(gx + 1, n_gx)
    gx_dn = lax.rem(gx + n_gx - 1, n_gx)
    gy_up = lax.rem(gy + 1, n_gy)
    gy_dn = lax.rem(gy + n_gy - 1, n_gy)

    def remote(src, dst, send, recv_sem, device):
        return pltpu.make_async_remote_copy(
            src_ref=src, dst_ref=dst, send_sem=send, recv_sem=recv_sem,
            device_id=device, device_id_type=MESH,
        )

    loads = []
    for f in range(2):
        for b in range(2):
            loads.append(pltpu.make_async_copy(
                fields[f].at[0, b],
                lev.at[0, f, pl.ds(RIM, EDGE), pl.ds(8 + EDGE * b, EDGE), :],
                in_sem.at[2 * f + b],
            ))
    for copy in loads:
        copy.start()

    barrier = pltpu.get_barrier_semaphore()

    @pl.loop(1, n_gy)
    def _(d):
        pl.semaphore_signal(barrier, inc=1, device_id=(gx, lax.rem(gy + d, n_gy)), device_id_type=MESH)

    for device in ((gx_up, gy), (gx_dn, gy), (gx_up, gy_up), (gx_up, gy_dn), (gx_dn, gy_up), (gx_dn, gy_dn)):
        pl.semaphore_signal(barrier, inc=1, device_id=device, device_id_type=MESH)

    for b in range(2):
        for c, values in enumerate((under_s, mobile_s, spread_s)):
            block = jnp.full((8, DEPTH), values[0, b], jnp.float32)
            own[b, c] = block
            coef[1, 1 + b, c] = block
    lane = lax.broadcasted_iota(jnp.int32, (8, DEPTH), 1)
    mine = jnp.where(lane == 2 * gy, owner_s[0, 0], 0) + jnp.where(lane == 2 * gy + 1, owner_s[0, 1], 0)
    ownid[...] = mine

    pl.semaphore_wait(barrier, n_gy + 5)

    halos = []
    for q in range(4):
        for f in range(2):
            rows = pl.ds(8 * q, 8)
            halos.append(remote(
                fields[f].at[0, 1, rows, pl.ds(EDGE - RIM, RIM), :], halo.at[q, f, 0],
                halo_send.at[0], y_sem.at[q], (gx, gy_up)))
            halos.append(remote(
                fields[f].at[0, 0, rows, pl.ds(0, RIM), :], halo.at[q, f, 1],
                halo_send.at[0], y_sem.at[q], (gx, gy_dn)))
        if q == 0:
            smalls = [
                remote(own.at[1], coef.at[1, 0], coef_send.at[0], coef_sem.at[0], (gx, gy_up)),
                remote(own.at[0], coef.at[1, 3], coef_send.at[1], coef_sem.at[1], (gx, gy_dn)),
                remote(own.at[pl.ds(0, 2)], coef.at[0, pl.ds(1, 2)], coef_send.at[2], coef_sem.at[2], (gx_up, gy)),
                remote(own.at[pl.ds(0, 2)], coef.at[2, pl.ds(1, 2)], coef_send.at[3], coef_sem.at[3], (gx_dn, gy)),
                remote(own.at[1], coef.at[0, 0], coef_send.at[4], coef_sem.at[4], (gx_up, gy_up)),
                remote(own.at[0], coef.at[0, 3], coef_send.at[5], coef_sem.at[5], (gx_up, gy_dn)),
                remote(own.at[1], coef.at[2, 0], coef_send.at[6], coef_sem.at[6], (gx_dn, gy_up)),
                remote(own.at[0], coef.at[2, 3], coef_send.at[7], coef_sem.at[7], (gx_dn, gy_dn)),
            ]
            for copy in halos + smalls:
                copy.start()
        else:
            for copy in halos[4 * q:]:
                copy.start()

    faces = []
    for f in range(2):
        for b in range(2):
            rows = pl.ds(8 + EDGE * b, EDGE)
            faces.append(remote(
                fields[f].at[0, b, pl.ds(EDGE - RIM, RIM)], lev.at[0, f, pl.ds(0, RIM), rows, :],
                halo_send.at[1], x_sem.at[0, f, b], (gx_up, gy)))
            faces.append(remote(
                fields[f].at[0, b, pl.ds(0, RIM)], lev.at[0, f, pl.ds(RIM + EDGE, RIM), rows, :],
                halo_send.at[1], x_sem.at[1, f, b], (gx_dn, gy)))
    for f in range(2):
        for xd, (planes, gx_to) in enumerate(((pl.ds(EDGE - RIM, RIM), gx_up), (pl.ds(0, RIM), gx_dn))):
            corner = halo.at[4, f]
            faces.append(remote(
                fields[f].at[0, 1, planes, pl.ds(EDGE - RIM, RIM), :], corner.at[0, pl.ds(RIM * xd, RIM)],
                halo_send.at[2], c_sem, (gx_to, gy_up)))
            faces.append(remote(
                fields[f].at[0, 0, planes, pl.ds(0, RIM), :], corner.at[1, pl.ds(RIM * xd, RIM)],
                halo_send.at[2], c_sem, (gx_to, gy_dn)))
    for copy in faces:
        copy.start()

    def id_copy(d):
        return remote(ownid, ids.at[gy], id_send, id_sem, (gx, lax.rem(gy + d, n_gy)))

    @pl.loop(1, n_gy)
    def _(d):
        id_copy(d).start()

    ids[gy] = mine

    first_lane = lane == 0
    last_lane = lane == DEPTH - 1

    def advance(level, i, q):
        near = []
        for f in range(2):
            low = 8 * q
            mid = lev[level, f, i, pl.ds(low, 8), :]
            lower_x = lev[level, f, i - 1, pl.ds(low, 8), :]
            upper_x = lev[level, f, i + 1, pl.ds(low, 8), :]
            lower_y = pltpu.roll(mid, 1, 0) if q == 0 else lev[level, f, i, pl.ds(low - 1, 8), :]
            upper_y = pltpu.roll(mid, 7, 0) if q == GROUPS - 1 else lev[level, f, i, pl.ds(low + 1, 8), :]
            lower_z = jnp.where(first_lane, mid, pltpu.roll(mid, 1, 1))
            upper_z = jnp.where(last_lane, mid, pltpu.roll(mid, DEPTH - 1, 1))
            near.append((mid, lower_x, upper_x, lower_y, upper_y, lower_z, upper_z))
        zone = (i + EDGE - RIM) // EDGE
        tile = (q + 3) // 4
        under = coef[zone, tile, 0]
        mobile = coef[zone, tile, 1]
        spread = coef[zone, tile, 2]
        p, xl, xu, yl, yu, zl, zu = near[0]
        u, sxl, sxu, syl, syu, szl, szu = near[1]
        dx, dy, dz = xu - xl, yu - yl, zu - zl
        dx2, dy2, dz2 = dx * dx, dy * dy, dz * dz
        two = dx2 + dy2 + dz2
        four = dx2 * dx2 + dy2 * dy2 + dz2 * dz2
        base = two + 4.0
        top = (4.0 * aniso_strength) * four - (3.0 * aniso_strength) * (two * two)
        aniso = 1.0 + top / (base * base)
        lap = (xu + xl) + (yu + yl) + (zu + zl) - 6.0 * p
        lap_u = (sxu + sxl) + (syu + syl) + (szu + szl) - 6.0 * u
        well = 1.0 - p * p
        change = mobile * (aniso * lap + p * well - coupling * (well * well) * (under + u))
        return p + change, u + spread * lap_u + 0.5 * change

    def middle(level, lo, hi):
        @pl.loop(lo, hi)
        def _(i):
            for q in range(GROUPS):
                new_p, new_u = advance(level, i, q)
                lev[level + 1, 0, i, pl.ds(8 * q, 8), :] = new_p
                lev[level + 1, 1, i, pl.ds(8 * q, 8), :] = new_u

    def last(lo, hi):
        @pl.loop(lo, hi)
        def _(i):
            t = (i - RIM) // 2
            h = lax.rem(i - RIM, 2)
            for q in range(1, GROUPS - 1):
                b, g = (q - 1) // 4, (q - 1) % 4
                new_p, new_u = advance(NSTEPS - 1, i, q)
                fin[0, b, t, h, pl.ds(8 * g, 8), :] = new_p
                fin[1, b, t, h, pl.ds(8 * g, 8), :] = new_u

    def spread_rims(lo, n, q, off):
        @pl.loop(0, n)
        def _(i):
            for f in range(2):
                lev[0, f, lo + i, pl.ds(RIM, RIM), :] = halo[q, f, 0, off + i]
                lev[0, f, lo + i, pl.ds(8 + 2 * EDGE, RIM), :] = halo[q, f, 1, off + i]

    def hop1_copy(c, d):
        to = lax.rem(gy + d, n_gy)
        f, g, h = lax.rem(to // 4, 2), lax.rem(to, 4), to // 8
        src = fin.at[f, :, pl.ds(2 * c, 2), h, pl.ds(pl.multiple_of(8 * g, 8), 8), :]
        return src, to

    def hop1(c):
        @pl.loop(1, n_gy)
        def _(d):
            src, to = hop1_copy(c, d)
            remote(src, recv[c].at[pl.ds(2 * gy, 2)], hop1_send.at[c], hop1_sem.at[c], (gx, to)).start()

        src, _ = hop1_copy(c, 0)
        pltpu.make_async_copy(src, recv[c].at[pl.ds(2 * gy, 2)], hop1_sem.at[c]).start()

    my_f, my_g, my_h = lax.rem(gy // 4, 2), lax.rem(gy, 4), gy // 8

    def hop2(c):
        pltpu.make_async_copy(recv[c], recv[c], hop1_sem.at[c]).wait()
        dst = out.at[my_f, :, pl.ds(2 * c, 2), my_h, pl.ds(pl.multiple_of(8 * my_g, 8), 8), :]

        def pick(d):
            to = lax.rem(gy + d, n_gy)
            for j in range(2):
                stage[c, to, j] = recv[c][table_s[j, to, 0]]
            return to

        @pl.loop(1, n_gy)
        def _(d):
            to = pick(d)
            remote(stage.at[c, to], dst, hop2_send.at[c], out_sem, (gx, to)).start()

        to = pick(0)
        pltpu.make_async_copy(stage.at[c, to], dst, out_sem).start()

    for copy in loads:
        copy.wait()
    for k in (0, 1):
        smalls[k].wait_recv()

    done = [5, 6, 7, 8]
    rims = 0
    for c in ORDER[:6]:
        top = 4 * c + 8
        limits = (min(top + 3, 35), min(top + 2, 34), top + 1, top)
        need = min((limits[0] - RIM) // 8 + 1, 4)
        while rims < need:
            pltpu.make_async_copy(halo.at[rims], halo.at[rims], y_sem.at[rims]).wait()
            spread_rims(RIM + 8 * rims, 8, rims, 0)
            rims += 1
        for level in range(NSTEPS - 1):
            middle(level, done[level], limits[level])
        last(done[3], limits[3])
        done = list(limits)
        hop1(c)
        if c == 1:
            others = ids.at[pl.ds(0, n_gy - 1)]
            pltpu.make_async_copy(others, others, id_sem).wait()
            total = ids[0]
            for s in range(1, n_gy):
                total = total + ids[s]
            both = jnp.concatenate([total, total], axis=0)
            lanes = lax.broadcasted_iota(jnp.int32, (n_gy, DEPTH), 1)
            wanted = gx * n_gy + lax.broadcasted_iota(jnp.int32, (n_gy, DEPTH), 0)
            match = (both == wanted) & (lanes < 2 * n_gy)
            least = jnp.min(jnp.where(match, lanes, 2 * n_gy - 1), axis=1, keepdims=True)
            most = jnp.max(jnp.where(match, lanes, 0), axis=1, keepdims=True)
            table_v[0] = jnp.broadcast_to(least, (n_gy, DEPTH))
            table_v[1] = jnp.broadcast_to(most, (n_gy, DEPTH))
            tab = pltpu.make_async_copy(table_v, table_s, tab_sem)
            tab.start()

    for copy in faces[:8]:
        copy.wait_recv()
    for k in range(2, 8):
        smalls[k].wait_recv()
    pltpu.make_async_copy(halo.at[4], halo.at[4], c_sem).wait()
    spread_rims(0, RIM, 4, 0)
    spread_rims(RIM + EDGE, RIM, 4, RIM)
    for level in range(NSTEPS - 1):
        middle(level, 1 + level, 5 + level)
    last(4, 8)
    hop1(0)
    for level in range(NSTEPS - 1):
        middle(level, 35 - level, 39 - level)
    last(32, 36)
    hop1(7)

    tab.wait()
    for c in ORDER:
        hop2(c)

    pltpu.make_async_copy(out, out, out_sem).wait()
    for k, sent in enumerate((halo.at[pl.ds(0, 4)], fin.at[0, 0], halo.at[4])):
        pltpu.make_async_copy(sent, sent, halo_send.at[k]).wait()
    for copy in smalls:
        copy.wait_send()
    others = ids.at[pl.ds(0, n_gy - 1)]
    pltpu.make_async_copy(others, others, id_send).wait()

    for c in range(CHUNKS):
        some = recv[c].at[pl.ds(0, 2 * n_gy - 2)]
        pltpu.make_async_copy(some, some, hop1_send.at[c]).wait()
        pltpu.make_async_copy(some, some, hop2_send.at[c]).wait()


def per_device(n_gx, n_gy, phase, solute, undercool, mobility, diffusivity, owner):
    smem = pl.BlockSpec(memory_space=pltpu.SMEM)
    hbm = pl.BlockSpec(memory_space=pl.ANY)
    f32 = jnp.float32
    dma = pltpu.SemaphoreType.DMA
    out = pl.pallas_call(
        functools.partial(kernel, n_gx, n_gy),
        out_shape=jax.ShapeDtypeStruct((2, 2, 16, 2, EDGE, DEPTH), f32),
        in_specs=[hbm, hbm, smem, smem, smem, smem],
        out_specs=hbm,
        scratch_shapes=[
            pltpu.VMEM((NSTEPS, 2, EDGE + 2 * RIM, 8 * GROUPS, DEPTH), f32),
            pltpu.VMEM((2, 2, 16, 2, EDGE, DEPTH), f32),
            pltpu.VMEM((5, 2, 2, 8, RIM, DEPTH), f32),
            pltpu.VMEM((3, 4, 3, 8, DEPTH), f32),
            pltpu.VMEM((2, 3, 8, DEPTH), f32),
            pltpu.VMEM((8, DEPTH), jnp.int32),
            pltpu.VMEM((n_gy, 8, DEPTH), jnp.int32),
            pltpu.VMEM((2, n_gy, DEPTH), jnp.int32),
            pltpu.SMEM((2, n_gy, DEPTH), jnp.int32),
            pltpu.VMEM((CHUNKS, n_gy, 2, 2, 8, DEPTH), f32),
        ]
        + [pltpu.VMEM((2 * n_gy, 2, 8, DEPTH), f32)] * CHUNKS
        + [
            dma((4,)), dma((4,)), dma((2, 2, 2)), dma(()), dma((8,)), dma(()), dma(()), dma((CHUNKS,)), dma(()),
            dma((3,)), dma((8,)), dma(()), dma((CHUNKS,)), dma((CHUNKS,)),
        ],
        compiler_params=pltpu.CompilerParams(
            collective_id=0, has_side_effects=True, vmem_limit_bytes=56 << 20
        ),
    )(phase, solute, undercool, mobility, diffusivity, owner)
    shape = (1, 2, EDGE, EDGE, DEPTH)
    return out[0].reshape(shape), out[1].reshape(shape)


def solution(mesh):
    in_specs = (
        P("gx", "gy", None, None, None),
        P("gx", "gy", None, None, None),
        P("gx", "gy"),
        P("gx", "gy"),
        P("gx", "gy"),
        P("gx", "gy"),
    )
    out_specs = (P(("gx", "gy"), None, None, None, None), P(("gx", "gy"), None, None, None, None))
    return jax.shard_map(
        functools.partial(per_device, mesh.shape["gx"], mesh.shape["gy"]),
        mesh=mesh, in_specs=in_specs, out_specs=out_specs, check_vma=False,
    )
```

time: 681 us -> 69.6 us (0.10)
  waiting for transfers between devices: 348 us -> 0 us
  local copies, waits for them, and re-layouts: 154 us -> 3.17 us
  starting transfers between devices: 93.2 us -> 0 us
  Pallas kernels: 0 us -> 65.7 us
  other arithmetic: 46.6 us -> 0 us
  blocking collectives: 36.6 us -> 0 us
    all_to_all x10 -> x0, waiting for transfers between devices: 305 us -> none  [the longest x1 108 us: per_device(): lax.all_to_all(place(solute_tiles, target, slots), 'gy', split_axis=0, co...]
    pallas_call x0 -> x1, Pallas kernels: none -> 65.7 us  [per_device(): pl.pallas_call(functools.partial(kernel, n_gx, n_gy), out_shape=jax.Shape...]
    all_to_all x10 -> x0, starting transfers between devices: 59.7 us -> none  [the longest x3 20.8 us: per_device(): lax.all_to_all(outgoing, 'gy', split_axis=0, concat_axis=0, tiled=True)]
    slice x35 -> x1, local copies, waits for them, and re-layouts: 57.6 us -> 3.17 us  [per_device(): return (out[0].reshape(shape), out[1].reshape(shape))]
    add x7 -> x0, other arithmetic: 44.7 us -> none  [step_cells(): new_solute = solute + spread * lap_solute + 0.5 * (new_phase - phase)]
    ppermute x16 -> x0, waiting for transfers between devices: 42.6 us -> none  [the longest x8 35.2 us: extended(): lax.ppermute(lax.slice_in_dim(block, block.shape[dim] - width, None, axis...]
    all_to_all x1 -> x0, blocking collectives: 36.6 us -> none  [per_device(): lax.all_to_all(place(boundary_faces(phase_owned, solute_owned), picked, s...]
    ppermute x16 -> x0, starting transfers between devices: 33.5 us -> none  [the longest x8 30.2 us: extended(): lax.ppermute(lax.slice_in_dim(block, 0, width, axis=dim), axis, backward)]
  transfers between devices with their start and end apart: 26 -> 0, of which waited for: 17 -> 0; matrix products, arithmetic and copies ran while one was open for 16% -> 0% of each run, Pallas kernels for 0% -> 0%
where the time goes in v1:
time: 69.6 us; the launch traced here: 69.5 us
  Pallas kernels  65.7 us (94%)
  local copies, waits for them, and re-layouts  3.17 us (5%)
    pallas_call x1, Pallas kernels, per_device(): pl.pallas_call(functools.partial(kernel, n_gx, n_gy), out_shape=jax.Shape...  65.7 us
    slice x1, local copies, waits for them, and re-layouts, per_device(): return (out[0].reshape(shape), out[1].reshape(shape))  3.17 us

profile of v1, /device:TPU:0, one launch (start us, length us, event | category | flops | bytes accessed | tf_op | source)
XLA Modules:
  0.0 69.5 jit_solution(916903431542181093)
XLA Ops:
  0.6 65.7 %shard_map.77 = f32[2,2,16,2,32,128]{5,4,3,2,1,0:T(8,128)} custom-call(f32[1,2,32,32,128]{4,3,2,1,0:T(8,128)} %phase.1, f32[1,2,32,32,128]{4,3,2,1,0:T(8,128)} %solute.1, f32[1,2]{1,0:T(1,128)} %under_s.1, f32[1,2]{1,0:T(1,128)} %mobile_s.1, f32[1,2]{1,0:T(1,128)} %spread_s.1, s32[1,2]{1,0:T(1,128)} %owner_s.1), custom_call_target="tpu_custom_call" | custom-call | tf_op jit(solution)/shard_map/pallas_call | solution.py:308
  66.3 3.2 %fusion = (f32[1,2,16,2,32,128]{5,4,3,2,1,0:T(8,128)}, f32[1,2,16,2,32,128]{5,4,3,2,1,0:T(8,128)}) fusion(f32[2,2,16,2,32,128]{5,4,3,2,1,0:T(8,128)} %shard_map.77), kind=kLoop, calls=%fused_computation | loop fusion | bytes 4194304 | tf_op jit(solution)/shard_map/slice | solution.py:335

commit v2 on v1

--- a/solution.py
+++ b/solution.py
@@ -307,7 +307,7 @@
     dma = pltpu.SemaphoreType.DMA
     out = pl.pallas_call(
         functools.partial(kernel, n_gx, n_gy),
-        out_shape=jax.ShapeDtypeStruct((2, 2, 16, 2, EDGE, DEPTH), f32),
+        out_shape=pltpu.VMEM((2, 2, 16, 2, EDGE, DEPTH), f32),
         in_specs=[hbm, hbm, smem, smem, smem, smem],
         out_specs=hbm,
         scratch_shapes=[

time: 69.6 us -> 68 us (0.977)
  local copies, waits for them, and re-layouts: 3.17 us -> 1.63 us
    slice x1, local copies, waits for them, and re-layouts: 3.17 us -> 1.63 us  [per_device(): return (out[0].reshape(shape), out[1].reshape(shape))]
where the time goes in v2:
time: 68 us; the launch traced here: 67.8 us
  Pallas kernels  65.6 us (96%)
  local copies, waits for them, and re-layouts  1.63 us (2%)
    pallas_call x1, Pallas kernels, per_device(): pl.pallas_call(functools.partial(kernel, n_gx, n_gy), out_shape=pltpu.VME...  65.6 us
    slice x1, local copies, waits for them, and re-layouts, per_device(): return (out[0].reshape(shape), out[1].reshape(shape))  1.63 us

profile of v2, /device:TPU:0, one launch (start us, length us, event | category | flops | bytes accessed | tf_op | source)
XLA Modules:
  0.0 67.8 jit_solution(8886228939407823965)
XLA Ops:
  0.6 65.6 %shard_map.77 = f32[2,2,16,2,32,128]{5,4,3,2,1,0:T(8,128)S(1)} custom-call(f32[1,2,32,32,128]{4,3,2,1,0:T(8,128)} %phase.1, f32[1,2,32,32,128]{4,3,2,1,0:T(8,128)} %solute.1, f32[1,2]{1,0:T(1,128)} %under_s.1, f32[1,2]{1,0:T(1,128)} %mobile_s.1, f32[1,2]{1,0:T(1,128)} %spread_s.1, s32[1,2]{1,0:T(1,128)} %owner_s.1), custom_call_target="tpu_custom_call" | custom-call | tf_op jit(solution)/shard_map/pallas_call | solution.py:308
  66.2 1.6 %fusion = (f32[1,2,16,2,32,128]{5,4,3,2,1,0:T(8,128)}, f32[1,2,16,2,32,128]{5,4,3,2,1,0:T(8,128)}) fusion(f32[2,2,16,2,32,128]{5,4,3,2,1,0:T(8,128)S(1)} %shard_map.77), kind=kLoop, calls=%fused_computation | loop fusion | bytes 4194304 | tf_op jit(solution)/shard_map/slice | solution.py:335

commit v3 on v2

v3 whole, which is shorter than its diff:
```python
import functools

import jax
import jax.numpy as jnp
from jax import lax
from jax.experimental import pallas as pl
from jax.experimental.pallas import tpu as pltpu
from jax.sharding import PartitionSpec as P

MESH = pl.DeviceIdType.MESH
NSTEPS = 4
RIM = 4
EDGE = 32
DEPTH = 128
GROUPS = 10
CHUNKS = 8
ORDER = (1, 2, 3, 4, 5, 6, 0, 7)

aniso_strength = 0.05
coupling = 2.0


def kernel(
    n_gx, n_gy,
    phase, solute, under_s, mobile_s, spread_s, owner_s,
    out,
    lev, fin, rim_y, rim_c, coef, own, ownid, ids, table_v, table_s, stage,
    recv0, recv1, recv2, recv3, recv4, recv5, recv6, recv7,
    in_sem, y_sem, x_sem, c_sem, coef_sem, id_sem, tab_sem, hop1_sem, out_sem,
    halo_send, coef_send, id_send, hop1_send, hop2_send,
):
    recv = (recv0, recv1, recv2, recv3, recv4, recv5, recv6, recv7)
    fields = (phase, solute)
    gx = lax.axis_index("gx")
    gy = lax.axis_index("gy")
    gx_up = lax.rem(gx + 1, n_gx)
    gx_dn = lax.rem(gx + n_gx - 1, n_gx)
    gy_up = lax.rem(gy + 1, n_gy)
    gy_dn = lax.rem(gy + n_gy - 1, n_gy)

    def remote(src, dst, send, recv_sem, device):
        return pltpu.make_async_remote_copy(
            src_ref=src, dst_ref=dst, send_sem=send, recv_sem=recv_sem,
            device_id=device, device_id_type=MESH,
        )

    loads = []
    for f in range(2):
        for b in range(2):
            loads.append(pltpu.make_async_copy(
                fields[f].at[0, b],
                lev.at[0, f, pl.ds(RIM, EDGE), pl.ds(8 + EDGE * b, EDGE), :],
                in_sem.at[2 * f + b],
            ))
    for copy in loads:
        copy.start()

    barrier = pltpu.get_barrier_semaphore()

    for d in range(1, 16):
        pl.semaphore_signal(barrier, inc=1, device_id=(gx, lax.rem(gy + d, n_gy)), device_id_type=MESH)

    for device in ((gx_up, gy), (gx_dn, gy), (gx_up, gy_up), (gx_up, gy_dn), (gx_dn, gy_up), (gx_dn, gy_dn)):
        pl.semaphore_signal(barrier, inc=1, device_id=device, device_id_type=MESH)

    for b in range(2):
        for c, values in enumerate((under_s, mobile_s, spread_s)):
            block = jnp.full((8, DEPTH), values[0, b], jnp.float32)
            own[b, c] = block
            coef[1, 1 + b, c] = block
    lane = lax.broadcasted_iota(jnp.int32, (8, DEPTH), 1)
    mine = jnp.where(lane == 2 * gy, owner_s[0, 0], 0) + jnp.where(lane == 2 * gy + 1, owner_s[0, 1], 0)
    ownid[...] = mine

    first_lane = lane == 0
    last_lane = lane == DEPTH - 1

    def advance(level, i, q):
        near = []
        for f in range(2):
            low = 8 * q
            mid = lev[level, f, i, pl.ds(low, 8), :]
            lower_x = lev[level, f, i - 1, pl.ds(low, 8), :]
            upper_x = lev[level, f, i + 1, pl.ds(low, 8), :]
            lower_y = pltpu.roll(mid, 1, 0) if q == 0 else lev[level, f, i, pl.ds(low - 1, 8), :]
            upper_y = pltpu.roll(mid, 7, 0) if q == GROUPS - 1 else lev[level, f, i, pl.ds(low + 1, 8), :]
            lower_z = jnp.where(first_lane, mid, pltpu.roll(mid, 1, 1))
            upper_z = jnp.where(last_lane, mid, pltpu.roll(mid, DEPTH - 1, 1))
            near.append((mid, lower_x, upper_x, lower_y, upper_y, lower_z, upper_z))
        zone = (i + EDGE - RIM) // EDGE
        tile = (q + 3) // 4
        under = coef[zone, tile, 0]
        mobile = coef[zone, tile, 1]
        spread = coef[zone, tile, 2]
        p, xl, xu, yl, yu, zl, zu = near[0]
        u, sxl, sxu, syl, syu, szl, szu = near[1]
        dx, dy, dz = xu - xl, yu - yl, zu - zl
        dx2, dy2, dz2 = dx * dx, dy * dy, dz * dz
        two = dx2 + dy2 + dz2
        four = dx2 * dx2 + dy2 * dy2 + dz2 * dz2
        base = two + 4.0
        top = (4.0 * aniso_strength) * four - (3.0 * aniso_strength) * (two * two)
        aniso = 1.0 + top / (base * base)
        lap = (xu + xl) + (yu + yl) + (zu + zl) - 6.0 * p
        lap_u = (sxu + sxl) + (syu + syl) + (szu + szl) - 6.0 * u
        well = 1.0 - p * p
        change = mobile * (aniso * lap + p * well - coupling * (well * well) * (under + u))
        return p + change, u + spread * lap_u + 0.5 * change

    def sweep(first, groups, last_groups, starts, pairs):
        @pl.loop(0, NSTEPS - 1)
        def _(level):
            @pl.loop(0, pairs(level))
            def _(n):
                for m in range(2):
                    i = starts(level) + 2 * n + m
                    for q in groups:
                        new_p, new_u = advance(level, i, q)
                        lev[level + 1, 0, i, pl.ds(8 * q, 8), :] = new_p
                        lev[level + 1, 1, i, pl.ds(8 * q, 8), :] = new_u

        @pl.loop(0, 2)
        def _(n):
            for m in range(2):
                i = first + RIM + 2 * n + m
                for q in last_groups:
                    b, g = (q - 1) // 4, (q - 1) % 4
                    new_p, new_u = advance(NSTEPS - 1, i, q)
                    fin[0, b, first // 2 + n, m, pl.ds(8 * g, 8), :] = new_p
                    fin[1, b, first // 2 + n, m, pl.ds(8 * g, 8), :] = new_u

    def sweep_inner(c, groups, last_groups):
        if c == 1:
            sweep(4, groups, last_groups, lambda level: 5 + level, lambda level: 5 - level)
        else:
            sweep(4 * c, groups, last_groups, lambda level: 4 * c + 7 - level, lambda level: 2)

    z, y = gy // 4, lax.rem(gy, 4)
    parity = lax.rem(z + y, 2)
    half = y // 2

    def piece(to_z, to_y, odd):
        side = to_y // 2
        g = 3 * side if odd else 1 + side
        return lax.rem(to_z, 2), pl.multiple_of(8 * g, 8), to_z // 2

    def hop1(c, odd):
        for dz in range(4):
            to_z = lax.rem(z + dz, 4)
            for m in range(2):
                to_y = 2 * lax.rem(half + m, 2) + lax.rem(to_z + odd + c, 2)
                f, row, h = piece(to_z, to_y, odd)
                src = fin.at[f, :, pl.ds(2 * c, 2), h, pl.ds(row, 8), :]
                dst = recv[c].at[pl.ds(2 * gy, 2)]

                def away():
                    remote(src, dst, hop1_send.at[c], hop1_sem.at[c], (gx, 4 * to_z + to_y)).start()

                if dz == 0 and m == 0:
                    pl.when(parity != (odd + c) % 2)(away)

                    @pl.when(parity == (odd + c) % 2)
                    def _():
                        pltpu.make_async_copy(src, dst, hop1_sem.at[c]).start()
                else:
                    away()

    my_f, my_h = lax.rem(z, 2), z // 2

    def hop2(c):
        pltpu.make_async_copy(recv[c], recv[c], hop1_sem.at[c]).wait()
        odd = lax.rem(parity + c, 2)
        row = pl.multiple_of(8 * ((1 - odd) * (1 + half) + odd * 3 * half), 8)
        dst = out.at[my_f, :, pl.ds(2 * c, 2), my_h, pl.ds(row, 8), :]
        for dz in range(4):
            for dy in range(4):
                to = 4 * lax.rem(z + dz, 4) + lax.rem(y + dy, 4)
                for j in range(2):
                    stage[c, to, j] = recv[c][table_s[j, to, 0]]
                if dz or dy:
                    remote(stage.at[c, to], dst, hop2_send.at[c], out_sem, (gx, to)).start()
                else:
                    pltpu.make_async_copy(stage.at[c, to], dst, out_sem).start()

    for copy in loads:
        copy.wait()
    inner, inner_last = range(1, GROUPS - 1), range(2, GROUPS - 2)
    sweep_inner(1, inner, inner_last)

    pl.semaphore_wait(barrier, n_gy + 5)

    for f in range(2):
        remote(fields[f].at[0, 1, :, pl.ds(EDGE - RIM, RIM), :], rim_y.at[f, 0], halo_send.at[0], y_sem, (gx, gy_up)).start()
        remote(fields[f].at[0, 0, :, pl.ds(0, RIM), :], rim_y.at[f, 1], halo_send.at[0], y_sem, (gx, gy_dn)).start()
    smalls = [
        remote(own.at[1], coef.at[1, 0], coef_send.at[0], coef_sem.at[0], (gx, gy_up)),
        remote(own.at[0], coef.at[1, 3], coef_send.at[1], coef_sem.at[1], (gx, gy_dn)),
        remote(own.at[pl.ds(0, 2)], coef.at[0, pl.ds(1, 2)], coef_send.at[2], coef_sem.at[2], (gx_up, gy)),
        remote(own.at[pl.ds(0, 2)], coef.at[2, pl.ds(1, 2)], coef_send.at[3], coef_sem.at[3], (gx_dn, gy)),
        remote(own.at[1], coef.at[0, 0], coef_send.at[4], coef_sem.at[4], (gx_up, gy_up)),
        remote(own.at[0], coef.at[0, 3], coef_send.at[5], coef_sem.at[5], (gx_up, gy_dn)),
        remote(own.at[1], coef.at[2, 0], coef_send.at[6], coef_sem.at[6], (gx_dn, gy_up)),
        remote(own.at[0], coef.at[2, 3], coef_send.at[7], coef_sem.at[7], (gx_dn, gy_dn)),
    ]
    for copy in smalls[:2]:
        copy.start()
    hop1(1, 0)

    faces = []
    for f in range(2):
        for b in range(2):
            rows = pl.ds(8 + EDGE * b, EDGE)
            faces.append(remote(
                fields[f].at[0, b, pl.ds(EDGE - RIM, RIM)], lev.at[0, f, pl.ds(0, RIM), rows, :],
                halo_send.at[1], x_sem.at[0, f, b], (gx_up, gy)))
            faces.append(remote(
                fields[f].at[0, b, pl.ds(0, RIM)], lev.at[0, f, pl.ds(RIM + EDGE, RIM), rows, :],
                halo_send.at[1], x_sem.at[1, f, b], (gx_dn, gy)))
    corners = []
    for f in range(2):
        for xd, (planes, gx_to) in enumerate(((pl.ds(EDGE - RIM, RIM), gx_up), (pl.ds(0, RIM), gx_dn))):
            corners.append(remote(
                fields[f].at[0, 1, planes, pl.ds(EDGE - RIM, RIM), :], rim_c.at[f, 0, pl.ds(RIM * xd, RIM)],
                halo_send.at[2], c_sem, (gx_to, gy_up)))
            corners.append(remote(
                fields[f].at[0, 0, planes, pl.ds(0, RIM), :], rim_c.at[f, 1, pl.ds(RIM * xd, RIM)],
                halo_send.at[2], c_sem, (gx_to, gy_dn)))
    for copy in faces + corners + smalls[2:]:
        copy.start()

    for d in range(1, 16):
        remote(ownid, ids.at[gy], id_send, id_sem, (gx, lax.rem(gy + d, n_gy))).start()
    ids[gy] = mine

    for c in range(2, 7):
        sweep_inner(c, inner, inner_last)
        hop1(c, 0)

    pltpu.make_async_copy(rim_y, rim_y, y_sem).wait()
    for copy in smalls[:2]:
        copy.wait_recv()

    def rims(source, lo, n, off):
        @pl.loop(0, n)
        def _(i):
            for f in range(2):
                lev[0, f, lo + i, pl.ds(RIM, RIM), :] = source[f, 0, off + i]
                lev[0, f, lo + i, pl.ds(8 + 2 * EDGE, RIM), :] = source[f, 1, off + i]

    rims(rim_y, RIM, EDGE, 0)
    for c in range(1, 7):
        sweep_inner(c, (0, 1, GROUPS - 2, GROUPS - 1), (1, GROUPS - 2))
        hop1(c, 1)

    others = ids.at[pl.ds(0, n_gy - 1)]
    pltpu.make_async_copy(others, others, id_sem).wait()
    total = ids[0]
    for s in range(1, 16):
        total = total + ids[s]
    both = jnp.concatenate([total, total], axis=0)
    lanes = lax.broadcasted_iota(jnp.int32, (n_gy, DEPTH), 1)
    wanted = gx * n_gy + lax.broadcasted_iota(jnp.int32, (n_gy, DEPTH), 0)
    match = (both == wanted) & (lanes < 2 * n_gy)
    least = jnp.min(jnp.where(match, lanes, 2 * n_gy - 1), axis=1, keepdims=True)
    most = jnp.max(jnp.where(match, lanes, 0), axis=1, keepdims=True)
    table_v[0] = jnp.broadcast_to(least, (n_gy, DEPTH))
    table_v[1] = jnp.broadcast_to(most, (n_gy, DEPTH))
    tab = pltpu.make_async_copy(table_v, table_s, tab_sem)
    tab.start()

    for copy in faces:
        copy.wait_recv()
    for copy in smalls[2:]:
        copy.wait_recv()
    pltpu.make_async_copy(rim_c, rim_c, c_sem).wait()
    rims(rim_c, 0, RIM, 0)
    rims(rim_c, RIM + EDGE, RIM, RIM)
    every, every_last = range(GROUPS), range(1, GROUPS - 1)
    for c, starts in ((0, lambda level: 1 + level), (7, lambda level: 35 - level)):
        sweep(4 * c, every, every_last, starts, lambda level: 2)
        hop1(c, 0)
        hop1(c, 1)

    tab.wait()
    for c in ORDER:
        hop2(c)

    pltpu.make_async_copy(out, out, out_sem).wait()
    for k, sent in enumerate((rim_y, fin.at[0, 0], rim_c)):
        pltpu.make_async_copy(sent, sent, halo_send.at[k]).wait()
    for copy in smalls:
        copy.wait_send()
    pltpu.make_async_copy(others, others, id_send).wait()
    for c in range(CHUNKS):
        some = recv[c].at[pl.ds(0, 2 * n_gy - 2)]
        pltpu.make_async_copy(some, some, hop1_send.at[c]).wait()
        pltpu.make_async_copy(some, some, hop2_send.at[c]).wait()


def per_device(n_gx, n_gy, phase, solute, undercool, mobility, diffusivity, owner):
    smem = pl.BlockSpec(memory_space=pltpu.SMEM)
    hbm = pl.BlockSpec(memory_space=pl.ANY)
    f32 = jnp.float32
    dma = pltpu.SemaphoreType.DMA
    out = pl.pallas_call(
        functools.partial(kernel, n_gx, n_gy),
        out_shape=pltpu.VMEM((2, 2, 16, 2, EDGE, DEPTH), f32),
        in_specs=[hbm, hbm, smem, smem, smem, smem],
        out_specs=hbm,
        scratch_shapes=[
            pltpu.VMEM((NSTEPS, 2, EDGE + 2 * RIM, 8 * GROUPS, DEPTH), f32),
            pltpu.VMEM((2, 2, 16, 2, EDGE, DEPTH), f32),
            pltpu.VMEM((2, 2, EDGE, RIM, DEPTH), f32),
            pltpu.VMEM((2, 2, 2 * RIM, RIM, DEPTH), f32),
            pltpu.VMEM((3, 4, 3, 8, DEPTH), f32),
            pltpu.VMEM((2, 3, 8, DEPTH), f32),
            pltpu.VMEM((8, DEPTH), jnp.int32),
            pltpu.VMEM((n_gy, 8, DEPTH), jnp.int32),
            pltpu.VMEM((2, n_gy, DEPTH), jnp.int32),
            pltpu.SMEM((2, n_gy, DEPTH), jnp.int32),
            pltpu.VMEM((CHUNKS, n_gy, 2, 2, 8, DEPTH), f32),
        ]
        + [pltpu.VMEM((2 * n_gy, 2, 8, DEPTH), f32)] * CHUNKS
        + [
            dma((4,)), dma(()), dma((2, 2, 2)), dma(()), dma((8,)), dma(()), dma(()), dma((CHUNKS,)), dma(()),
            dma((3,)), dma((8,)), dma(()), dma((CHUNKS,)), dma((CHUNKS,)),
        ],
        compiler_params=pltpu.CompilerParams(
            collective_id=0, has_side_effects=True, vmem_limit_bytes=56 << 20
        ),
    )(phase, solute, undercool, mobility, diffusivity, owner)
    shape = (1, 2, EDGE, EDGE, DEPTH)
    return out[0].reshape(shape), out[1].reshape(shape)


def solution(mesh):
    in_specs = (
        P("gx", "gy", None, None, None),
        P("gx", "gy", None, None, None),
        P("gx", "gy"),
        P("gx", "gy"),
        P("gx", "gy"),
        P("gx", "gy"),
    )
    out_specs = (P(("gx", "gy"), None, None, None, None), P(("gx", "gy"), None, None, None, None))
    return jax.shard_map(
        functools.partial(per_device, mesh.shape["gx"], mesh.shape["gy"]),
        mesh=mesh, in_specs=in_specs, out_specs=out_specs, check_vma=False,
    )
```

time: 68 us -> 65.3 us (0.960); the launches traced: 67.8 us -> 64.4 us
  Pallas kernels: 65.6 us -> 62.2 us
    pallas_call x1, Pallas kernels: 65.6 us -> 62.2 us  [per_device(): pl.pallas_call(functools.partial(kernel, n_gx, n_gy), out_shape=pltpu.VME...]
where the time goes in v3:
time: 65.3 us; the launch traced here: 64.4 us
  Pallas kernels  62.2 us (95%)
  local copies, waits for them, and re-layouts  1.63 us (2%)
    pallas_call x1, Pallas kernels, per_device(): pl.pallas_call(functools.partial(kernel, n_gx, n_gy), out_shape=pltpu.VME...  62.2 us
    slice x1, local copies, waits for them, and re-layouts, per_device(): return (out[0].reshape(shape), out[1].reshape(shape))  1.63 us

profile of v3, /device:TPU:0, one launch (start us, length us, event | category | flops | bytes accessed | tf_op | source)
XLA Modules:
  0.0 64.4 jit_solution(6366005114184545149)
XLA Ops:
  0.6 62.2 %shard_map.77 = f32[2,2,16,2,32,128]{5,4,3,2,1,0:T(8,128)S(1)} custom-call(f32[1,2,32,32,128]{4,3,2,1,0:T(8,128)} %phase.1, f32[1,2,32,32,128]{4,3,2,1,0:T(8,128)} %solute.1, f32[1,2]{1,0:T(1,128)} %under_s.1, f32[1,2]{1,0:T(1,128)} %mobile_s.1, f32[1,2]{1,0:T(1,128)} %spread_s.1, s32[1,2]{1,0:T(1,128)} %owner_s.1), custom_call_target="tpu_custom_call" | custom-call | tf_op jit(solution)/shard_map/pallas_call | solution.py:305
  62.8 1.6 %fusion = (f32[1,2,16,2,32,128]{5,4,3,2,1,0:T(8,128)}, f32[1,2,16,2,32,128]{5,4,3,2,1,0:T(8,128)}) fusion(f32[2,2,16,2,32,128]{5,4,3,2,1,0:T(8,128)S(1)} %shard_map.77), kind=kLoop, calls=%fused_computation | loop fusion | bytes 4194304 | tf_op jit(solution)/shard_map/slice | solution.py:333

commit v4 on v3

--- a/solution.py
+++ b/solution.py
@@ -24,7 +24,7 @@
     n_gx, n_gy,
     phase, solute, under_s, mobile_s, spread_s, owner_s,
     out,
-    lev, fin, rim_y, rim_c, coef, own, ownid, ids, table_v, table_s, stage,
+    lev, fin, rim_y, rim_c, coef, packs, own, ownid, ids, table_v, table_s, stage,
     recv0, recv1, recv2, recv3, recv4, recv5, recv6, recv7,
     in_sem, y_sem, x_sem, c_sem, coef_sem, id_sem, tab_sem, hop1_sem, out_sem,
     halo_send, coef_send, id_send, hop1_send, hop2_send,
@@ -63,14 +63,17 @@
     for device in ((gx_up, gy), (gx_dn, gy), (gx_up, gy_up), (gx_up, gy_dn), (gx_dn, gy_up), (gx_dn, gy_dn)):
         pl.semaphore_signal(barrier, inc=1, device_id=device, device_id_type=MESH)
 
+    line = lax.broadcasted_iota(jnp.int32, (8, DEPTH), 0)
     for b in range(2):
+        packed = jnp.zeros((8, DEPTH), jnp.float32)
         for c, values in enumerate((under_s, mobile_s, spread_s)):
             block = jnp.full((8, DEPTH), values[0, b], jnp.float32)
-            own[b, c] = block
+            packed = jnp.where(line == c, block, packed)
             coef[1, 1 + b, c] = block
+        own[b] = packed
     lane = lax.broadcasted_iota(jnp.int32, (8, DEPTH), 1)
     mine = jnp.where(lane == 2 * gy, owner_s[0, 0], 0) + jnp.where(lane == 2 * gy + 1, owner_s[0, 1], 0)
-    ownid[...] = mine
+    ownid[...] = mine[:1]
 
     first_lane = lane == 0
     last_lane = lane == DEPTH - 1
@@ -130,10 +133,11 @@
                     fin[1, b, first // 2 + n, m, pl.ds(8 * g, 8), :] = new_u
 
     def sweep_inner(c, groups, last_groups):
-        if c == 1:
-            sweep(4, groups, last_groups, lambda level: 5 + level, lambda level: 5 - level)
-        else:
-            sweep(4 * c, groups, last_groups, lambda level: 4 * c + 7 - level, lambda level: 2)
+        opening = 1 - (c + 3) // 5
+        sweep(
+            4 * c, groups, last_groups,
+            lambda level: 4 * c + 7 - level - opening * (6 - 2 * level), lambda level: 2 + opening * (3 - level),
+        )
 
     z, y = gy // 4, lax.rem(gy, 4)
     parity = lax.rem(z + y, 2)
@@ -182,30 +186,25 @@
                 else:
                     pltpu.make_async_copy(stage.at[c, to], dst, out_sem).start()
 
-    for copy in loads:
-        copy.wait()
-    inner, inner_last = range(1, GROUPS - 1), range(2, GROUPS - 2)
-    sweep_inner(1, inner, inner_last)
-
     pl.semaphore_wait(barrier, n_gy + 5)
 
     for f in range(2):
         remote(fields[f].at[0, 1, :, pl.ds(EDGE - RIM, RIM), :], rim_y.at[f, 0], halo_send.at[0], y_sem, (gx, gy_up)).start()
         remote(fields[f].at[0, 0, :, pl.ds(0, RIM), :], rim_y.at[f, 1], halo_send.at[0], y_sem, (gx, gy_dn)).start()
     smalls = [
-        remote(own.at[1], coef.at[1, 0], coef_send.at[0], coef_sem.at[0], (gx, gy_up)),
-        remote(own.at[0], coef.at[1, 3], coef_send.at[1], coef_sem.at[1], (gx, gy_dn)),
-        remote(own.at[pl.ds(0, 2)], coef.at[0, pl.ds(1, 2)], coef_send.at[2], coef_sem.at[2], (gx_up, gy)),
-        remote(own.at[pl.ds(0, 2)], coef.at[2, pl.ds(1, 2)], coef_send.at[3], coef_sem.at[3], (gx_dn, gy)),
-        remote(own.at[1], coef.at[0, 0], coef_send.at[4], coef_sem.at[4], (gx_up, gy_up)),
-        remote(own.at[0], coef.at[0, 3], coef_send.at[5], coef_sem.at[5], (gx_up, gy_dn)),
-        remote(own.at[1], coef.at[2, 0], coef_send.at[6], coef_sem.at[6], (gx_dn, gy_up)),
-        remote(own.at[0], coef.at[2, 3], coef_send.at[7], coef_sem.at[7], (gx_dn, gy_dn)),
+        remote(own.at[1], packs.at[1, 0], coef_send.at[0], coef_sem.at[0], (gx, gy_up)),
+        remote(own.at[0], packs.at[1, 3], coef_send.at[1], coef_sem.at[1], (gx, gy_dn)),
+        remote(own.at[pl.ds(0, 2)], packs.at[0, pl.ds(1, 2)], coef_send.at[2], coef_sem.at[2], (gx_up, gy)),
+        remote(own.at[pl.ds(0, 2)], packs.at[2, pl.ds(1, 2)], coef_send.at[3], coef_sem.at[3], (gx_dn, gy)),
+        remote(own.at[1], packs.at[0, 0], coef_send.at[4], coef_sem.at[4], (gx_up, gy_up)),
+        remote(own.at[0], packs.at[0, 3], coef_send.at[5], coef_sem.at[5], (gx_up, gy_dn)),
+        remote(own.at[1], packs.at[2, 0], coef_send.at[6], coef_sem.at[6], (gx_dn, gy_up)),
+        remote(own.at[0], packs.at[2, 3], coef_send.at[7], coef_sem.at[7], (gx_dn, gy_dn)),
     ]
     for copy in smalls[:2]:
         copy.start()
-    hop1(1, 0)
-
+    for copy in loads:
+        copy.wait()
     faces = []
     for f in range(2):
         for b in range(2):
@@ -225,20 +224,30 @@
             corners.append(remote(
                 fields[f].at[0, 0, planes, pl.ds(0, RIM), :], rim_c.at[f, 1, pl.ds(RIM * xd, RIM)],
                 halo_send.at[2], c_sem, (gx_to, gy_dn)))
+
     for copy in faces + corners + smalls[2:]:
         copy.start()
-
     for d in range(1, 16):
         remote(ownid, ids.at[gy], id_send, id_sem, (gx, lax.rem(gy + d, n_gy))).start()
-    ids[gy] = mine
-
-    for c in range(2, 7):
-        sweep_inner(c, inner, inner_last)
-        hop1(c, 0)
+
+    @pl.loop(1, 7)
+    def _(c):
+        sweep_inner(c, range(1, GROUPS - 1), range(2, GROUPS - 2))
+        for k in range(1, 7):
+            pl.when(c == k)(functools.partial(hop1, k, 0))
+
+    ids[gy] = mine[:1]
 
     pltpu.make_async_copy(rim_y, rim_y, y_sem).wait()
     for copy in smalls[:2]:
         copy.wait_recv()
+
+    def unpack(zone, tiles):
+        for tile in tiles:
+            for c in range(3):
+                coef[zone, tile, c] = jnp.broadcast_to(packs[zone, tile, pl.ds(c, 1), :], (8, DEPTH))
+
+    unpack(1, (0, 3))
 
     def rims(source, lo, n, off):
         @pl.loop(0, n)
@@ -248,16 +257,19 @@
                 lev[0, f, lo + i, pl.ds(8 + 2 * EDGE, RIM), :] = source[f, 1, off + i]
 
     rims(rim_y, RIM, EDGE, 0)
-    for c in range(1, 7):
+
+    @pl.loop(1, 7)
+    def _(c):
         sweep_inner(c, (0, 1, GROUPS - 2, GROUPS - 1), (1, GROUPS - 2))
-        hop1(c, 1)
+        for k in range(1, 7):
+            pl.when(c == k)(functools.partial(hop1, k, 1))
 
     others = ids.at[pl.ds(0, n_gy - 1)]
     pltpu.make_async_copy(others, others, id_sem).wait()
     total = ids[0]
     for s in range(1, 16):
         total = total + ids[s]
-    both = jnp.concatenate([total, total], axis=0)
+    both = jnp.broadcast_to(total, (n_gy, DEPTH))
     lanes = lax.broadcasted_iota(jnp.int32, (n_gy, DEPTH), 1)
     wanted = gx * n_gy + lax.broadcasted_iota(jnp.int32, (n_gy, DEPTH), 0)
     match = (both == wanted) & (lanes < 2 * n_gy)
@@ -272,14 +284,23 @@
         copy.wait_recv()
     for copy in smalls[2:]:
         copy.wait_recv()
+    unpack(0, range(4))
+    unpack(2, range(4))
     pltpu.make_async_copy(rim_c, rim_c, c_sem).wait()
     rims(rim_c, 0, RIM, 0)
     rims(rim_c, RIM + EDGE, RIM, RIM)
-    every, every_last = range(GROUPS), range(1, GROUPS - 1)
-    for c, starts in ((0, lambda level: 1 + level), (7, lambda level: 35 - level)):
-        sweep(4 * c, every, every_last, starts, lambda level: 2)
-        hop1(c, 0)
-        hop1(c, 1)
+
+    @pl.loop(0, 2)
+    def _(e):
+        sweep(
+            28 * e, range(GROUPS), range(1, GROUPS - 1),
+            lambda level: 1 + 34 * e + level * (1 - 2 * e), lambda level: 2,
+        )
+        for k in range(2):
+            @pl.when(e == k)
+            def _():
+                hop1(7 * k, 0)
+                hop1(7 * k, 1)
 
     tab.wait()
     for c in ORDER:
@@ -313,9 +334,10 @@
             pltpu.VMEM((2, 2, EDGE, RIM, DEPTH), f32),
             pltpu.VMEM((2, 2, 2 * RIM, RIM, DEPTH), f32),
             pltpu.VMEM((3, 4, 3, 8, DEPTH), f32),
-            pltpu.VMEM((2, 3, 8, DEPTH), f32),
-            pltpu.VMEM((8, DEPTH), jnp.int32),
-            pltpu.VMEM((n_gy, 8, DEPTH), jnp.int32),
+            pltpu.VMEM((3, 4, 8, DEPTH), f32),
+            pltpu.VMEM((2, 8, DEPTH), f32),
+            pltpu.VMEM((1, DEPTH), jnp.int32),
+            pltpu.VMEM((n_gy, 1, DEPTH), jnp.int32),
             pltpu.VMEM((2, n_gy, DEPTH), jnp.int32),
             pltpu.SMEM((2, n_gy, DEPTH), jnp.int32),
             pltpu.VMEM((CHUNKS, n_gy, 2, 2, 8, DEPTH), f32),

time: 65.3 us -> 63.7 us (0.975)
  Pallas kernels: 62.2 us -> 60.6 us
    pallas_call x1, Pallas kernels: 62.2 us -> 60.6 us  [per_device(): pl.pallas_call(functools.partial(kernel, n_gx, n_gy), out_shape=pltpu.VME...]
where the time goes in v4:
time: 63.7 us; the launch traced here: 62.9 us
  Pallas kernels  60.6 us (95%)
  local copies, waits for them, and re-layouts  1.63 us (3%)
  between operations  0.64 us (1%)
    pallas_call x1, Pallas kernels, per_device(): pl.pallas_call(functools.partial(kernel, n_gx, n_gy), out_shape=pltpu.VME...  60.6 us
    slice x1, local copies, waits for them, and re-layouts, per_device(): return (out[0].reshape(shape), out[1].reshape(shape))  1.63 us

profile of v4, /device:TPU:0, one launch (start us, length us, event | category | flops | bytes accessed | tf_op | source)
XLA Modules:
  0.0 62.9 jit_solution(4831594523667052006)
XLA Ops:
  0.6 60.6 %shard_map.77 = f32[2,2,16,2,32,128]{5,4,3,2,1,0:T(8,128)S(1)} custom-call(f32[1,2,32,32,128]{4,3,2,1,0:T(8,128)} %phase.1, f32[1,2,32,32,128]{4,3,2,1,0:T(8,128)} %solute.1, f32[1,2]{1,0:T(1,128)} %under_s.1, f32[1,2]{1,0:T(1,128)} %mobile_s.1, f32[1,2]{1,0:T(1,128)} %spread_s.1, s32[1,2]{1,0:T(1,128)} %owner_s.1), custom_call_target="tpu_custom_call" | custom-call | tf_op jit(solution)/shard_map/pallas_call | solution.py:326
  61.3 1.6 %fusion = (f32[1,2,16,2,32,128]{5,4,3,2,1,0:T(8,128)}, f32[1,2,16,2,32,128]{5,4,3,2,1,0:T(8,128)}) fusion(f32[2,2,16,2,32,128]{5,4,3,2,1,0:T(8,128)S(1)} %shard_map.77), kind=kLoop, calls=%fused_computation | loop fusion | bytes 4194304 | tf_op jit(solution)/shard_map/slice | solution.py:355

commit v5 on v4

--- a/solution.py
+++ b/solution.py
@@ -22,8 +22,9 @@
 
 def kernel(
     n_gx, n_gy,
-    phase, solute, under_s, mobile_s, spread_s, owner_s,
+    phase, solute, under, mobile, spread_in, owner,
     out,
+    under_s, mobile_s, spread_s, owner_s, small_sem,
     lev, fin, rim_y, rim_c, coef, packs, own, ownid, ids, table_v, table_s, stage,
     recv0, recv1, recv2, recv3, recv4, recv5, recv6, recv7,
     in_sem, y_sem, x_sem, c_sem, coef_sem, id_sem, tab_sem, hop1_sem, out_sem,
@@ -52,17 +53,26 @@
                 lev.at[0, f, pl.ds(RIM, EDGE), pl.ds(8 + EDGE * b, EDGE), :],
                 in_sem.at[2 * f + b],
             ))
+    scalars = [
+        pltpu.make_async_copy(src, dst, small_sem.at[k])
+        for k, (src, dst) in enumerate(((under, under_s), (mobile, mobile_s), (spread_in, spread_s), (owner, owner_s)))
+    ]
+    for copy in scalars:
+        copy.start()
+
+    barrier = pltpu.get_barrier_semaphore()
+
+    for d in range(1, 16):
+        pl.semaphore_signal(barrier, inc=1, device_id=(gx, lax.rem(gy + d, n_gy)), device_id_type=MESH)
+
+    for device in ((gx_up, gy), (gx_dn, gy), (gx_up, gy_up), (gx_up, gy_dn), (gx_dn, gy_up), (gx_dn, gy_dn)):
+        pl.semaphore_signal(barrier, inc=1, device_id=device, device_id_type=MESH)
+
     for copy in loads:
         copy.start()
 
-    barrier = pltpu.get_barrier_semaphore()
-
-    for d in range(1, 16):
-        pl.semaphore_signal(barrier, inc=1, device_id=(gx, lax.rem(gy + d, n_gy)), device_id_type=MESH)
-
-    for device in ((gx_up, gy), (gx_dn, gy), (gx_up, gy_up), (gx_up, gy_dn), (gx_dn, gy_up), (gx_dn, gy_dn)):
-        pl.semaphore_signal(barrier, inc=1, device_id=device, device_id_type=MESH)
-
+    for copy in scalars:
+        copy.wait()
     line = lax.broadcasted_iota(jnp.int32, (8, DEPTH), 0)
     for b in range(2):
         packed = jnp.zeros((8, DEPTH), jnp.float32)
@@ -319,16 +329,16 @@
 
 
 def per_device(n_gx, n_gy, phase, solute, undercool, mobility, diffusivity, owner):
-    smem = pl.BlockSpec(memory_space=pltpu.SMEM)
     hbm = pl.BlockSpec(memory_space=pl.ANY)
     f32 = jnp.float32
     dma = pltpu.SemaphoreType.DMA
     out = pl.pallas_call(
         functools.partial(kernel, n_gx, n_gy),
         out_shape=pltpu.VMEM((2, 2, 16, 2, EDGE, DEPTH), f32),
-        in_specs=[hbm, hbm, smem, smem, smem, smem],
+        in_specs=[hbm] * 6,
         out_specs=hbm,
         scratch_shapes=[
+            pltpu.SMEM((1, 2), f32), pltpu.SMEM((1, 2), f32), pltpu.SMEM((1, 2), f32), pltpu.SMEM((1, 2), jnp.int32), dma((4,)),
             pltpu.VMEM((NSTEPS, 2, EDGE + 2 * RIM, 8 * GROUPS, DEPTH), f32),
             pltpu.VMEM((2, 2, 16, 2, EDGE, DEPTH), f32),
             pltpu.VMEM((2, 2, EDGE, RIM, DEPTH), f32),

time: 63.7 us -> 63.1 us (level)
    pallas_call x1, Pallas kernels: 60.6 us -> 60 us  [per_device(): pl.pallas_call(functools.partial(kernel, n_gx, n_gy), out_shape=pltpu.VME...]
where the time goes in v5:
time: 63.1 us; the launch traced here: 62.2 us
  Pallas kernels  60 us (95%)
  local copies, waits for them, and re-layouts  1.63 us (3%)
  between operations  0.64 us (1%)
    pallas_call x1, Pallas kernels, per_device(): pl.pallas_call(functools.partial(kernel, n_gx, n_gy), out_shape=pltpu.VME...  60 us
    slice x1, local copies, waits for them, and re-layouts, per_device(): return (out[0].reshape(shape), out[1].reshape(shape))  1.63 us

profile of v5, /device:TPU:0, one launch (start us, length us, event | category | flops | bytes accessed | tf_op | source)
XLA Modules:
  0.0 62.2 jit_solution(4860688325573062400)
XLA Ops:
  0.6 60.0 %shard_map.77 = f32[2,2,16,2,32,128]{5,4,3,2,1,0:T(8,128)S(1)} custom-call(f32[1,2,32,32,128]{4,3,2,1,0:T(8,128)} %phase.1, f32[1,2,32,32,128]{4,3,2,1,0:T(8,128)} %solute.1, f32[1,2]{1,0:T(1,128)} %under.1, f32[1,2]{1,0:T(1,128)} %mobile.1, f32[1,2]{1,0:T(1,128)} %spread_in.1, s32[1,2]{1,0:T(1,128)} %owner.1), custom_call_target="tpu_custom_call" | custom-call | tf_op jit(solution)/shard_map/pallas_call | solution.py:335
  60.6 1.6 %fusion = (f32[1,2,16,2,32,128]{5,4,3,2,1,0:T(8,128)}, f32[1,2,16,2,32,128]{5,4,3,2,1,0:T(8,128)}) fusion(f32[2,2,16,2,32,128]{5,4,3,2,1,0:T(8,128)S(1)} %shard_map.77), kind=kLoop, calls=%fused_computation | loop fusion | bytes 4194304 | tf_op jit(solution)/shard_map/slice | solution.py:365

commit v6 on v5

--- a/solution.py
+++ b/solution.py
@@ -186,15 +186,20 @@
         odd = lax.rem(parity + c, 2)
         row = pl.multiple_of(8 * ((1 - odd) * (1 + half) + odd * 3 * half), 8)
         dst = out.at[my_f, :, pl.ds(2 * c, 2), my_h, pl.ds(row, 8), :]
-        for dz in range(4):
-            for dy in range(4):
-                to = 4 * lax.rem(z + dz, 4) + lax.rem(y + dy, 4)
-                for j in range(2):
-                    stage[c, to, j] = recv[c][table_s[j, to, 0]]
-                if dz or dy:
-                    remote(stage.at[c, to], dst, hop2_send.at[c], out_sem, (gx, to)).start()
-                else:
-                    pltpu.make_async_copy(stage.at[c, to], dst, out_sem).start()
+        def pick(d):
+            to = lax.rem(gy + d, n_gy)
+            for j in range(2):
+                stage[c, to, j] = recv[c][table_s[j, to, 0]]
+            return to
+
+        @pl.loop(0, 5)
+        def _(n):
+            for m in range(3):
+                to = pick(3 * n + m + 1)
+                remote(stage.at[c, to], dst, hop2_send.at[c], out_sem, (gx, to)).start()
+
+        to = pick(0)
+        pltpu.make_async_copy(stage.at[c, to], dst, out_sem).start()
 
     pl.semaphore_wait(barrier, n_gy + 5)
 
@@ -242,7 +247,7 @@
 
     @pl.loop(1, 7)
     def _(c):
-        sweep_inner(c, range(1, GROUPS - 1), range(2, GROUPS - 2))
+        sweep_inner(c, range(1, GROUPS - 1), (2, 3, 6, 7))
         for k in range(1, 7):
             pl.when(c == k)(functools.partial(hop1, k, 0))
 
@@ -270,9 +275,31 @@
 
     @pl.loop(1, 7)
     def _(c):
-        sweep_inner(c, (0, 1, GROUPS - 2, GROUPS - 1), (1, GROUPS - 2))
+        sweep_inner(c, (0, 1, GROUPS - 2, GROUPS - 1), (1, 4, 5, 8))
         for k in range(1, 7):
             pl.when(c == k)(functools.partial(hop1, k, 1))
+
+    for copy in faces:
+        copy.wait_recv()
+    for copy in smalls[2:]:
+        copy.wait_recv()
+    unpack(0, range(4))
+    unpack(2, range(4))
+    pltpu.make_async_copy(rim_c, rim_c, c_sem).wait()
+    rims(rim_c, 0, RIM, 0)
+    rims(rim_c, RIM + EDGE, RIM, RIM)
+
+    @pl.loop(0, 2)
+    def _(e):
+        sweep(
+            28 * e, range(GROUPS), range(1, GROUPS - 1),
+            lambda level: 1 + 34 * e + level * (1 - 2 * e), lambda level: 2,
+        )
+        for k in range(2):
+            @pl.when(e == k)
+            def _():
+                hop1(7 * k, 0)
+                hop1(7 * k, 1)
 
     others = ids.at[pl.ds(0, n_gy - 1)]
     pltpu.make_async_copy(others, others, id_sem).wait()
@@ -289,28 +316,6 @@
     table_v[1] = jnp.broadcast_to(most, (n_gy, DEPTH))
     tab = pltpu.make_async_copy(table_v, table_s, tab_sem)
     tab.start()
-
-    for copy in faces:
-        copy.wait_recv()
-    for copy in smalls[2:]:
-        copy.wait_recv()
-    unpack(0, range(4))
-    unpack(2, range(4))
-    pltpu.make_async_copy(rim_c, rim_c, c_sem).wait()
-    rims(rim_c, 0, RIM, 0)
-    rims(rim_c, RIM + EDGE, RIM, RIM)
-
-    @pl.loop(0, 2)
-    def _(e):
-        sweep(
-            28 * e, range(GROUPS), range(1, GROUPS - 1),
-            lambda level: 1 + 34 * e + level * (1 - 2 * e), lambda level: 2,
-        )
-        for k in range(2):
-            @pl.when(e == k)
-            def _():
-                hop1(7 * k, 0)
-                hop1(7 * k, 1)
 
     tab.wait()
     for c in ORDER:

time: 63.1 us -> 63.2 us (level)
  no operation moved by 1% of the time
where the time goes in v6:
time: 63.2 us; the launch traced here: 62.2 us
  Pallas kernels  59.9 us (95%)
  local copies, waits for them, and re-layouts  1.63 us (3%)
  between operations  0.64 us (1%)
    pallas_call x1, Pallas kernels, per_device(): pl.pallas_call(functools.partial(kernel, n_gx, n_gy), out_shape=pltpu.VME...  59.9 us
    slice x1, local copies, waits for them, and re-layouts, per_device(): return (out[0].reshape(shape), out[1].reshape(shape))  1.63 us

profile of v6, /device:TPU:0, one launch (start us, length us, event | category | flops | bytes accessed | tf_op | source)
XLA Modules:
  0.0 62.2 jit_solution(12606470432203639311)
XLA Ops:
  0.6 59.9 %shard_map.77 = f32[2,2,16,2,32,128]{5,4,3,2,1,0:T(8,128)S(1)} custom-call(f32[1,2,32,32,128]{4,3,2,1,0:T(8,128)} %phase.1, f32[1,2,32,32,128]{4,3,2,1,0:T(8,128)} %solute.1, f32[1,2]{1,0:T(1,128)} %under.1, f32[1,2]{1,0:T(1,128)} %mobile.1, f32[1,2]{1,0:T(1,128)} %spread_in.1, s32[1,2]{1,0:T(1,128)} %owner.1), custom_call_target="tpu_custom_call" | custom-call | tf_op jit(solution)/shard_map/pallas_call | solution.py:340
  60.6 1.6 %fusion = (f32[1,2,16,2,32,128]{5,4,3,2,1,0:T(8,128)}, f32[1,2,16,2,32,128]{5,4,3,2,1,0:T(8,128)}) fusion(f32[2,2,16,2,32,128]{5,4,3,2,1,0:T(8,128)S(1)} %shard_map.77), kind=kLoop, calls=%fused_computation | loop fusion | bytes 4194304 | tf_op jit(solution)/shard_map/slice | solution.py:370

commit v7 on v6

--- a/solution.py
+++ b/solution.py
@@ -123,14 +123,18 @@
     def sweep(first, groups, last_groups, starts, pairs):
         @pl.loop(0, NSTEPS - 1)
         def _(level):
-            @pl.loop(0, pairs(level))
-            def _(n):
-                for m in range(2):
-                    i = starts(level) + 2 * n + m
+            def planes(start, count):
+                for m in range(count):
+                    i = start + m
                     for q in groups:
                         new_p, new_u = advance(level, i, q)
                         lev[level + 1, 0, i, pl.ds(8 * q, 8), :] = new_p
                         lev[level + 1, 1, i, pl.ds(8 * q, 8), :] = new_u
+
+            if pairs is None:
+                planes(starts(level), 4)
+            else:
+                pl.loop(0, pairs(level))(lambda n: planes(starts(level) + 2 * n, 2))
 
         @pl.loop(0, 2)
         def _(n):
@@ -293,7 +297,7 @@
     def _(e):
         sweep(
             28 * e, range(GROUPS), range(1, GROUPS - 1),
-            lambda level: 1 + 34 * e + level * (1 - 2 * e), lambda level: 2,
+            lambda level: 1 + 34 * e + level * (1 - 2 * e), None,
         )
         for k in range(2):
             @pl.when(e == k)

time: 63.2 us -> 63.2 us (level)
  no operation moved by 1% of the time
where the time goes in v7:
time: 63.2 us; the launch traced here: 62.2 us
  Pallas kernels  59.9 us (95%)
  local copies, waits for them, and re-layouts  1.63 us (3%)
  between operations  0.64 us (1%)
    pallas_call x1, Pallas kernels, per_device(): pl.pallas_call(functools.partial(kernel, n_gx, n_gy), out_shape=pltpu.VME...  59.9 us
    slice x1, local copies, waits for them, and re-layouts, per_device(): return (out[0].reshape(shape), out[1].reshape(shape))  1.63 us

profile of v7, /device:TPU:0, one launch (start us, length us, event | category | flops | bytes accessed | tf_op | source)
XLA Modules:
  0.0 62.2 jit_solution(17349774845345702552)
XLA Ops:
  0.6 59.9 %shard_map.77 = f32[2,2,16,2,32,128]{5,4,3,2,1,0:T(8,128)S(1)} custom-call(f32[1,2,32,32,128]{4,3,2,1,0:T(8,128)} %phase.1, f32[1,2,32,32,128]{4,3,2,1,0:T(8,128)} %solute.1, f32[1,2]{1,0:T(1,128)} %under.1, f32[1,2]{1,0:T(1,128)} %mobile.1, f32[1,2]{1,0:T(1,128)} %spread_in.1, s32[1,2]{1,0:T(1,128)} %owner.1), custom_call_target="tpu_custom_call" | custom-call | tf_op jit(solution)/shard_map/pallas_call | solution.py:344
  60.6 1.6 %fusion = (f32[1,2,16,2,32,128]{5,4,3,2,1,0:T(8,128)}, f32[1,2,16,2,32,128]{5,4,3,2,1,0:T(8,128)}) fusion(f32[2,2,16,2,32,128]{5,4,3,2,1,0:T(8,128)S(1)} %shard_map.77), kind=kLoop, calls=%fused_computation | loop fusion | bytes 4194304 | tf_op jit(solution)/shard_map/slice | solution.py:374
